TPU v7x, 128 devices: a whole 4x4x4 slice. The times are simulated.
128 devices in a mesh: band: 8 (over z_hi, y), blk: 16 (over x, z_lo, core).
Axes of the slice: x: 4, y: 4, z: 4 (z_hi: 2, z_lo: 2; z = z_hi * 2 + z_lo), core: 2. Of those that a mesh axis runs over, the one named last changes fastest.
Arguments:
- volt: bfloat16 [2, 2048, 110592], P(None, ('blk', 'band')), may hold values from -6 to 6
- band_chans: int32 [8, 8], replicated, may hold values from 0 to 4095, as said below
- band_count: int32 [8], replicated, may hold values from 1 to 8, as said below
Outputs:
- visibility: bfloat16 [2, 8, 8, 2048, 2048], P(None, 'band', None, 'blk')
Inputs may be any that keep to these rules, and one draw needn't show every extreme that they name: `band_chans`: all entries are distinct channels; slots at or beyond a band group's count name channels too and are not correlated. `band_count`: one band group has exactly 8 live slots in every draw.
All inputs are finite; a program needn't handle non-finite values.
Results may differ from a plain program's by a relative error of at most 0.0057.
Values may be sent and summed in bfloat16 or wider, within the bound.
A program may use at most 192 MiB of HBM per device.

v0:
```python
import math

import jax
import jax.numpy as jnp
import numpy as np
from jax import lax
from jax.experimental import pallas as pl
from jax.experimental.pallas import tpu as pltpu
from jax.sharding import PartitionSpec as P

C = 4096
TAPS = 16
NSPEC = 12
FRAMES = NSPEC + TAPS - 1
EL = 16
LANES = 128
BANDS = 8
SLOTS = 8
GROUPS = 4
GROUP_W = C // GROUPS
CHUNK = 256
N_CHUNK = C // CHUNK
MESH = pl.DeviceIdType.MESH
F32, BF16 = jnp.float32, jnp.bfloat16


def taper_table():
    idx = np.arange(TAPS * C, dtype=np.float64)
    centre = (idx + 0.5) / C - TAPS / 2.0
    window = 0.5 - 0.5 * np.cos(2.0 * math.pi * (idx + 0.5) / (TAPS * C))
    prototype = np.sinc(centre) * window
    prototype = prototype / np.sqrt(np.sum(prototype * prototype))
    return prototype.reshape(TAPS, C).astype(np.float32)


def cos_sin(turns):
    shifted = turns + 512
    quarter = (shifted >> 10) & 3
    x = ((shifted & 1023) - 512).astype(F32) * (2.0 * math.pi / 4096.0)
    x2 = x * x
    s = x * (1.0 + x2 * (-1.0 / 6 + x2 * (1.0 / 120 + x2 * (-1.0 / 5040 + x2 * (1.0 / 362880)))))
    c = 1.0 + x2 * (-0.5 + x2 * (1.0 / 24 + x2 * (-1.0 / 720 + x2 * (1.0 / 40320))))
    odd = (quarter & 1) == 1
    cc, ss = jnp.where(odd, s, c), jnp.where(odd, c, s)
    cc = jnp.where((quarter == 1) | (quarter == 2), -cc, cc)
    ss = jnp.where(quarter >= 2, -ss, ss)
    return cc, ss


def split(y):
    hi = y.astype(BF16)
    return hi, (y - hi.astype(F32)).astype(BF16)


def front_kernel(
    volt, chans, taper, z, samples, base_c, base_s, step_c, step_s, table, lhs_a, lhs_b, total, sems
):
    def fetch(group, frame):
        return pltpu.make_async_copy(
            volt.at[:, :, pl.ds(frame * C + group * GROUP_W, GROUP_W)],
            samples.at[group, frame],
            sems.at[group],
        )

    for group in range(GROUPS):
        for frame in range(FRAMES):
            fetch(group, frame).start()

    lane = lax.broadcasted_iota(jnp.int32, (8, LANES), 1)
    key = ((lane >> 4) << 3) + (lane & 7)
    row = jnp.zeros((8, LANES), jnp.int32)
    for g in range(BANDS):
        for s in range(SLOTS):
            row = jnp.where(key == g * SLOTS + s, chans[g, s], row)
    quarter_turn = ((lane[:1] >> 3) & 1) * 1024
    row = row[:1]
    inner = lax.broadcasted_iota(jnp.int32, (LANES, LANES), 0)
    c0, s0 = cos_sin((inner * row + quarter_turn) & 4095)
    base_c[...] = c0
    base_s[...] = s0
    outer = lax.broadcasted_iota(jnp.int32, (C // LANES, LANES), 0) * LANES
    c1, s1 = cos_sin((outer * row) & 4095)
    step_c[...] = c1
    step_s[...] = s1

    def build(chunk, carry):
        for part in range(CHUNK // LANES):
            a = chunk * (CHUNK // LANES) + part
            ca, sa = step_c[pl.ds(a, 1), :], step_s[pl.ds(a, 1), :]
            cb, sb = base_c[...], base_s[...]
            for comp, value in ((0, ca * cb - sa * sb), (1, sa * cb + ca * sb)):
                hi, lo = split(value)
                rows = slice(comp * CHUNK + part * LANES, comp * CHUNK + (part + 1) * LANES)
                table[chunk, rows, :LANES] = hi
                table[chunk, rows, LANES:] = lo
        return carry

    lax.fori_loop(0, N_CHUNK, build, 0)

    def weigh(chunk, lhs):
        group = chunk // (GROUP_W // CHUNK)
        for part in range(CHUNK // LANES):
            k = pl.multiple_of(chunk * CHUNK + part * LANES, LANES)
            in_group = pl.multiple_of(k - group * GROUP_W, LANES)
            taps = [
                jnp.broadcast_to(taper[p : p + 1, pl.ds(k, LANES)], (EL, LANES))
                for p in range(TAPS)
            ]
            for comp in range(2):
                column = slice(comp * CHUNK + part * LANES, comp * CHUNK + (part + 1) * LANES)
                acc = [None] * NSPEC
                for f in range(FRAMES):
                    x = samples[group, f, comp, :, pl.ds(in_group, LANES)].astype(F32)
                    for t in range(max(0, f - TAPS + 1), min(NSPEC - 1, f) + 1):
                        term = taps[f - t] * x
                        acc[t] = term if acc[t] is None else acc[t] + term
                    if f >= TAPS - 1:
                        t = f - TAPS + 1
                        hi, lo = split(acc[t])
                        lhs[t * EL : (t + 1) * EL, column] = hi
                        lhs[NSPEC * EL + t * EL : NSPEC * EL + (t + 1) * EL, column] = lo
                        acc[t] = None

    def transform(chunk, lhs):
        total[...] += jnp.dot(lhs[...], table[chunk], preferred_element_type=F32)

    def wait_group(group):
        pltpu.make_async_copy(samples.at[group], samples.at[group], sems.at[group]).wait()

    total[...] = jnp.zeros_like(total)
    lhs_b[...] = jnp.zeros_like(lhs_b)

    per_group = GROUP_W // CHUNK

    def two_chunks(i, carry):
        first = i * 2
        weigh(first, lhs_a)
        transform(lax.max(first - 1, 0), lhs_b)
        weigh(first + 1, lhs_b)
        transform(first, lhs_a)
        return carry

    for group in range(GROUPS):
        wait_group(group)
        lax.fori_loop(group * per_group // 2, (group + 1) * per_group // 2, two_chunks, 0)
    transform(N_CHUNK - 1, lhs_b)

    rows = NSPEC * EL
    y = (total[:rows, LANES:] + total[rows:, :LANES]) + (
        total[rows:, LANES:] + total[:rows, :LANES]
    )
    place = lax.broadcasted_iota(jnp.int32, (EL, LANES), 1) >> 4
    for g in range(BANDS):
        for tile in range(2):
            out = jnp.zeros((EL, LANES), F32)
            for t in range(tile * 8, min(tile * 8 + 8, NSPEC)):
                moved = y[t * EL : (t + 1) * EL]
                shift = (t - g) * 16 % LANES
                if shift:
                    moved = pltpu.roll(moved, shift, 1)
                out = jnp.where(place == t - tile * 8, moved, out)
            z[g, :, tile * LANES : (tile + 1) * LANES] = out.astype(BF16)


def front(volt, chans):
    vmem = pl.BlockSpec(memory_space=pltpu.VMEM)
    return pl.pallas_call(
        front_kernel,
        out_shape=jax.ShapeDtypeStruct((BANDS, EL, 2 * LANES), BF16),
        in_specs=[
            pl.BlockSpec(memory_space=pl.ANY),
            pl.BlockSpec(memory_space=pltpu.SMEM),
            vmem,
        ],
        out_specs=vmem,
        scratch_shapes=[
            pltpu.VMEM((GROUPS, FRAMES, 2, EL, GROUP_W), BF16),
            pltpu.VMEM((LANES, LANES), F32),
            pltpu.VMEM((LANES, LANES), F32),
            pltpu.VMEM((C // LANES, LANES), F32),
            pltpu.VMEM((C // LANES, LANES), F32),
            pltpu.VMEM((N_CHUNK, 2 * CHUNK, 2 * LANES), BF16),
            pltpu.VMEM((2 * NSPEC * EL, 2 * CHUNK), BF16),
            pltpu.VMEM((2 * NSPEC * EL, 2 * CHUNK), BF16),
            pltpu.VMEM((2 * NSPEC * EL, 2 * LANES), F32),
            pltpu.SemaphoreType.DMA((GROUPS,)),
        ],
        compiler_params=pltpu.CompilerParams(vmem_limit_bytes=48 * 2**20),
        name="filterbank",
    )(volt, chans, jnp.asarray(taper_table()))


def share_kernel(
    n_band, n_blk, z, x, own, ct_send, ct_recv, ag_send, ag_recv, fw_send, fw_recv, here
):
    g, b = lax.axis_index("band"), lax.axis_index("blk")
    core, near, along = b % 2, b // 2 % 2, b // 4
    n_along = n_blk // 4
    sibling = b + 1 - 2 * core
    el = z.shape[1]
    block = el * n_band

    def chip(d_along, d_near):
        return ((along + d_along) % n_along * 2 + (near + d_near) % 2) * 2 + core

    hops = [(da, dn) for da in range(n_along) for dn in range(2) if (da, dn) != (0, 0)]
    barrier = pltpu.get_barrier_semaphore()
    peers = [((g + d) % n_band, b) for d in range(1, n_band)]
    peers += [(g, chip(*hop)) for hop in hops] + [(g, sibling)]
    for peer in peers:
        pl.semaphore_signal(barrier, inc=1, device_id=peer, device_id_type=MESH)
    pl.semaphore_wait(barrier, len(peers))

    mine = pl.ds(pl.multiple_of(g * el, el), el)
    turns = []
    for d in range(1, n_band):
        to = (g + d) % n_band
        turns.append(
            pltpu.make_async_remote_copy(
                z.at[to], own.at[mine], ct_send.at[d], ct_recv.at[d], (to, b), MESH
            )
        )
        turns[-1].start()
    keep = pltpu.make_async_copy(z.at[g], own.at[mine], here.at[0])
    keep.start()
    keep.wait()
    for turn in turns:
        turn.wait()

    def rows(owner):
        return pl.ds(pl.multiple_of(owner * block, block), block)

    sends = []
    for n, hop in enumerate(hops):
        sends.append(
            pltpu.make_async_remote_copy(
                own, x.at[rows(b)], ag_send.at[n], ag_recv.at[n], (g, chip(*hop)), MESH
            )
        )
        sends[-1].start()
    last = len(hops)
    passed = [
        pltpu.make_async_remote_copy(
            own, x.at[rows(b)], fw_send.at[last], fw_recv.at[last], (g, sibling), MESH
        )
    ]
    passed[0].start()
    keep = pltpu.make_async_copy(own, x.at[rows(b)], here.at[1])
    keep.start()
    for n, (da, dn) in enumerate(hops):
        sends[n].wait_recv()
        owner = chip(n_along - da, 2 - dn)
        passed.append(
            pltpu.make_async_remote_copy(
                x.at[rows(owner)],
                x.at[rows(owner)],
                fw_send.at[n],
                fw_recv.at[n],
                (g, sibling),
                MESH,
            )
        )
        passed[-1].start()
    keep.wait()
    for send in sends:
        send.wait_send()
    for one in passed:
        one.wait()


def share(z, n_band, n_blk):
    el, width = z.shape[1], z.shape[2]
    vmem = pl.BlockSpec(memory_space=pltpu.VMEM)
    dma = pltpu.SemaphoreType.DMA

    def body(*refs):
        share_kernel(n_band, n_blk, *refs)

    return pl.pallas_call(
        body,
        out_shape=jax.ShapeDtypeStruct((el * n_band * n_blk, width), BF16),
        in_specs=[vmem],
        out_specs=vmem,
        scratch_shapes=[
            pltpu.VMEM((el * n_band, width), BF16),
            dma((n_band,)),
            dma((n_band,)),
            dma((n_blk // 2,)),
            dma((n_blk // 2,)),
            dma((n_blk // 2,)),
            dma((n_blk // 2,)),
            dma((2,)),
        ],
        compiler_params=pltpu.CompilerParams(collective_id=0, has_side_effects=True),
        name="corner_turn_and_gather",
    )(z)


COLUMNS = 256


def correlate_kernel(x, count, out, lhs):
    j = pl.program_id(0)
    block = out.shape[3]

    @pl.when(j == 0)
    def _():
        b = lax.axis_index("blk")
        live = count[lax.axis_index("band")]
        lane = lax.broadcasted_iota(jnp.int32, (block, LANES), 1)
        slot = lane & 7
        is_real = (lane & 8) == 0
        for tile in range(2):
            cols = slice(tile * LANES, (tile + 1) * LANES)
            own = x[pl.ds(pl.multiple_of(b * block, block), block), cols].astype(F32)
            turned = jnp.where(
                is_real, pltpu.roll(own, LANES - 8, 1), -pltpu.roll(own, 8, 1)
            )
            own = jnp.where(slot < live, own, 0.0)
            turned = jnp.where(slot < live, turned, 0.0)
            if tile == 1:
                used = lane < (NSPEC - 8) * 16
                own, turned = jnp.where(used, own, 0.0), jnp.where(used, turned, 0.0)
            for s in range(SLOTS):
                for part, value in ((0, own), (1, turned)):
                    at = (part * SLOTS + s) * block
                    lhs[at : at + block, cols] = jnp.where(slot == s, value, 0.0).astype(BF16)

    right = x[pl.ds(pl.multiple_of(j * COLUMNS, COLUMNS), COLUMNS), :]
    for part in range(2):
        for s in range(SLOTS):
            at = (part * SLOTS + s) * block
            y = lax.dot_general(
                lhs[at : at + block, :], right, (((1,), (1,)), ((), ())), preferred_element_type=F32
            )
            out[part, 0, s] = (y * (1.0 / NSPEC)).astype(BF16)


def correlate(x, count, n_band, n_blk):
    everyone = x.shape[0]
    block = everyone // n_blk
    return pl.pallas_call(
        correlate_kernel,
        grid=(everyone // COLUMNS,),
        out_shape=jax.ShapeDtypeStruct((2, 1, SLOTS, block, everyone), BF16),
        in_specs=[
            pl.BlockSpec(memory_space=pltpu.VMEM),
            pl.BlockSpec(memory_space=pltpu.SMEM),
        ],
        out_specs=pl.BlockSpec((2, 1, SLOTS, block, COLUMNS), lambda j: (0, 0, 0, 0, j)),
        scratch_shapes=[pltpu.VMEM((2 * SLOTS * block, x.shape[1]), BF16)],
        compiler_params=pltpu.CompilerParams(vmem_limit_bytes=32 * 2**20),
        name="correlate",
    )(x, count)


def solution(mesh):
    n_band, n_blk = mesh.shape["band"], mesh.shape["blk"]

    def local(volt, band_chans, band_count):
        z = front(volt, band_chans)
        x = share(z, n_band, n_blk)
        return correlate(x, band_count, n_band, n_blk)

    return jax.shard_map(
        local,
        mesh=mesh,
        in_specs=(P(None, ("blk", "band"), None), P(), P()),
        out_specs=P(None, "band", None, "blk", None),
        check_vma=False,
    )
```

profile of v0, /device:TPU:1, one launch (start us, length us, event | category | flops | bytes accessed | tf_op | source)
XLA Modules:
  0.0 48.8 jit_solution(17843223316143373729)
XLA Ops:
  0.0 0.0 copy-start.2
  0.0 0.9 %copy-done.2 = f32[16,4096]{1,0:T(8,128)S(1)} copy-done((f32[16,4096]{1,0:T(8,128)S(1)}, f32[16,4096]{1,0:T(8,128)}, u32[]{:S(2)}) %copy-start.2) | copy-done | bytes 262168
  1.0 0.0 copy-start.3
  1.0 0.7 %copy-done.3 = s32[8,8]{1,0:T(8,128)S(1)} copy-done((s32[8,8]{1,0:T(8,128)S(1)}, s32[8,8]{1,0:T(8,128)}, u32[]{:S(2)}) %copy-start.3) | copy-done | bytes 280
  1.6 0.0 copy-start.4
  1.6 13.7 %filterbank.1.refs_0_ = bf16[8,16,256]{2,1,0:T(8,128)(2,1)S(1)} custom-call(bf16[2,16,110592]{2,1,0:T(8,128)(2,1)} %volt.1, s32[8,8]{1,0:T(8,128)S(1)} %copy-done.3, f32[16,4096]{1,0:T(8,128)S(1)} %copy-done.2), custom_call_target="tpu_custom_call" | custom-call | tf_op jit(solution)/shard_map/filterbank/pallas_call | solution.py:167
  15.3 0.0 copy-start.1
  15.3 0.6 %copy-done.1 = bf16[8,16,256]{2,1,0:T(8,128)(2,1)} copy-done((bf16[8,16,256]{2,1,0:T(8,128)(2,1)}, bf16[8,16,256]{2,1,0:T(8,128)(2,1)S(1)}, u32[]{:S(2)}) %copy-start.1) | copy-done | bytes 65560
  15.9 23.0 %corner_turn_and_gather.1.x = bf16[2048,256]{1,0:T(8,128)(2,1)} custom-call(bf16[8,16,256]{2,1,0:T(8,128)(2,1)} %copy-done.1), custom_call_target="tpu_custom_call" | custom-call | tf_op jit(solution)/shard_map/corner_turn_and_gather/pallas_call | solution.py:279
  38.9 0.0 copy-done.4
  38.9 0.0 copy-start
  39.0 1.2 %copy-done = bf16[2048,256]{1,0:T(8,128)(2,1)S(1)} copy-done((bf16[2048,256]{1,0:T(8,128)(2,1)S(1)}, bf16[2048,256]{1,0:T(8,128)(2,1)}, u32[]{:S(2)}) %copy-start) | copy-done | bytes 1048600
  40.2 8.7 %correlate.1 = bf16[2,1,8,128,2048]{4,3,2,1,0:T(8,128)(2,1)} custom-call(bf16[2048,256]{1,0:T(8,128)(2,1)S(1)} %copy-done, s32[8]{0:T(128)S(1)} %copy-done.4), custom_call_target="tpu_custom_call" | custom-call | tf_op jit(solution)/shard_map/correlate/pallas_call | solution.py:342
Async XLA Ops:
  0.0 0.9 %copy-start.2 = (f32[16,4096]{1,0:T(8,128)S(1)}, f32[16,4096]{1,0:T(8,128)}, u32[]{:S(2)}) copy-start(f32[16,4096]{1,0:T(8,128)} %constant.2.clone.taper) | copy-start | bytes 786436
  1.0 0.7 %copy-start.3 = (s32[8,8]{1,0:T(8,128)S(1)}, s32[8,8]{1,0:T(8,128)}, u32[]{:S(2)}) copy-start(s32[8,8]{1,0:T(8,128)} %chans.1) | copy-start | bytes 772
  1.6 37.3 %copy-start.4 = (s32[8]{0:T(128)S(1)}, s32[8]{0:T(128)}, u32[]{:S(2)}) copy-start(s32[8]{0:T(128)} %count.1) | copy-start | bytes 100
  15.3 0.6 %copy-start.1 = (bf16[8,16,256]{2,1,0:T(8,128)(2,1)}, bf16[8,16,256]{2,1,0:T(8,128)(2,1)S(1)}, u32[]{:S(2)}) copy-start(bf16[8,16,256]{2,1,0:T(8,128)(2,1)S(1)} %filterbank.1.refs_0_) | copy-start | bytes 196612
  38.9 1.2 %copy-start = (bf16[2048,256]{1,0:T(8,128)(2,1)S(1)}, bf16[2048,256]{1,0:T(8,128)(2,1)}, u32[]{:S(2)}) copy-start(bf16[2048,256]{1,0:T(8,128)(2,1)} %corner_turn_and_gather.1.x) | copy-start | bytes 3145732
where the time goes:
time: 49.1 us; the launch traced here: 48.8 us
  Pallas kernels  45.3 us (92%)
  local copies, waits for them, and re-layouts  3.48 us (7%)
    pallas_call x1, Pallas kernels, share(): pl.pallas_call(body, out_shape=jax.ShapeDtypeStruct((el * n_band * n_blk,...  23 us
    pallas_call x1, Pallas kernels, front(): pl.pallas_call(front_kernel, out_shape=jax.ShapeDtypeStruct((BANDS, EL, 2...  13.7 us
    pallas_call x1, Pallas kernels, correlate(): pl.pallas_call(correlate_kernel, grid=(everyone // COLUMNS,), out_shape=j...  8.67 us
    unnamed x10, local copies, waits for them, and re-layouts  3.48 us

commit v1 on v0

v1 whole, which is shorter than its diff:
```python
import math

import jax
import jax.numpy as jnp
import numpy as np
from jax import lax
from jax.experimental import pallas as pl
from jax.experimental.pallas import tpu as pltpu
from jax.sharding import PartitionSpec as P

C = 4096
TAPS = 16
NSPEC = 12
FRAMES = NSPEC + TAPS - 1
EL = 16
LANES = 128
BANDS = 8
SLOTS = 8
GROUPS = 4
GROUP_W = C // GROUPS
CHUNK = 512
N_CENTRE = 4
N_CHUNK = C // CHUNK
MESH = pl.DeviceIdType.MESH
F32, BF16 = jnp.float32, jnp.bfloat16


def taper_table():
    idx = np.arange(TAPS * C, dtype=np.float64)
    centre = (idx + 0.5) / C - TAPS / 2.0
    window = 0.5 - 0.5 * np.cos(2.0 * math.pi * (idx + 0.5) / (TAPS * C))
    prototype = np.sinc(centre) * window
    prototype = prototype / np.sqrt(np.sum(prototype * prototype))
    return prototype.reshape(TAPS, C).astype(np.float32)


def cos_sin(turns):
    shifted = turns + 512
    quarter = (shifted >> 10) & 3
    x = ((shifted & 1023) - 512).astype(F32) * (2.0 * math.pi / 4096.0)
    x2 = x * x
    s = x * (1.0 + x2 * (-1.0 / 6 + x2 * (1.0 / 120 + x2 * (-1.0 / 5040 + x2 * (1.0 / 362880)))))
    c = 1.0 + x2 * (-0.5 + x2 * (1.0 / 24 + x2 * (-1.0 / 720 + x2 * (1.0 / 40320))))
    odd = (quarter & 1) == 1
    cc, ss = jnp.where(odd, s, c), jnp.where(odd, c, s)
    cc = jnp.where((quarter == 1) | (quarter == 2), -cc, cc)
    ss = jnp.where(quarter >= 2, -ss, ss)
    return cc, ss


def split(y):
    hi = y.astype(BF16)
    return hi, (y - hi.astype(F32)).astype(BF16)


CENTRE = tuple(range(TAPS // 2 - N_CENTRE // 2, TAPS // 2 + N_CENTRE // 2))
OUTER = tuple(p for p in range(TAPS) if p not in CENTRE)
ROWS = 2 * NSPEC * EL


def front_kernel(
    n_band, n_blk, volt, chans_hbm, taper_hbm, x, chans, taper, small_sems, samples, base_c, base_s,
    step_c, step_s, table, lhs_a, lhs_b, total, sems, z, held, ct_send, ct_recv, ag_send, ag_recv,
    fw_send, fw_recv, here,
):
    greet(n_band, n_blk)
    def fetch(group, frame):
        return pltpu.make_async_copy(
            volt.at[:, :, pl.ds(frame * C + group * GROUP_W, GROUP_W)],
            samples.at[group, frame],
            sems.at[group],
        )

    small = [
        pltpu.make_async_copy(chans_hbm, chans, small_sems.at[0]),
        pltpu.make_async_copy(taper_hbm, taper, small_sems.at[1]),
    ]
    for copy in small:
        copy.start()
    for group in range(GROUPS):
        for frame in range(FRAMES):
            fetch(group, frame).start()
    small[0].wait()

    lane = lax.broadcasted_iota(jnp.int32, (8, LANES), 1)
    key = ((lane >> 4) << 3) + (lane & 7)
    row = jnp.zeros((8, LANES), jnp.int32)
    for g in range(BANDS):
        for s in range(SLOTS):
            row = jnp.where(key == g * SLOTS + s, chans[g, s], row)
    quarter_turn = ((lane[:1] >> 3) & 1) * 1024
    row = row[:1]
    inner = lax.broadcasted_iota(jnp.int32, (LANES, LANES), 0)
    c0, s0 = cos_sin((inner * row + quarter_turn) & 4095)
    base_c[...] = c0
    base_s[...] = s0
    outer = lax.broadcasted_iota(jnp.int32, (C // LANES, LANES), 0) * LANES
    c1, s1 = cos_sin((outer * row) & 4095)
    step_c[...] = c1
    step_s[...] = s1

    def build(chunk, carry):
        for part in range(CHUNK // LANES):
            a = chunk * (CHUNK // LANES) + part
            ca, sa = step_c[pl.ds(a, 1), :], step_s[pl.ds(a, 1), :]
            hi, lo = split(ca * base_c[...] - sa * base_s[...])
            rows = slice(part * LANES, (part + 1) * LANES)
            table[chunk, rows, :LANES] = hi
            table[chunk, rows, LANES:] = lo
        return carry

    lax.fori_loop(0, N_CHUNK, build, 0)

    def weigh(chunk, lhs):
        group = chunk // (GROUP_W // CHUNK)
        for part in range(CHUNK // LANES):
            k = pl.multiple_of(chunk * CHUNK + part * LANES, LANES)
            in_group = pl.multiple_of(k - group * GROUP_W, LANES)
            taps = [
                jnp.broadcast_to(taper[p : p + 1, pl.ds(k, LANES)], (EL, LANES))
                for p in range(TAPS)
            ]
            taps = [taps[p] if p in CENTRE else taps[p].astype(BF16) for p in range(TAPS)]
            column = slice(part * LANES, (part + 1) * LANES)
            for comp in range(2):
                side, mid = [None] * NSPEC, [None] * NSPEC
                for f in range(FRAMES):
                    x = samples[group, f, comp, :, pl.ds(in_group, LANES)]
                    wide = x.astype(F32)
                    for t in range(max(0, f - TAPS + 1), min(NSPEC - 1, f) + 1):
                        p = f - t
                        if p in CENTRE:
                            term = taps[p] * wide
                            mid[t] = term if mid[t] is None else mid[t] + term
                        else:
                            term = taps[p] * x
                            side[t] = term if side[t] is None else side[t] + term
                    if f >= TAPS - 1:
                        t = f - TAPS + 1
                        hi, lo = split(mid[t] + side[t].astype(F32))
                        at = (comp * NSPEC + t) * EL
                        lhs[at : at + EL, column] = hi
                        lhs[ROWS + at : ROWS + at + EL, column] = lo

    def transform(chunk, lhs):
        r = jnp.dot(lhs[...], table[chunk], preferred_element_type=F32)
        total[...] += (r[:ROWS, LANES:] + r[ROWS:, :LANES]) + r[:ROWS, :LANES]

    def wait_group(group):
        pltpu.make_async_copy(samples.at[group], samples.at[group], sems.at[group]).wait()

    small[1].wait()
    total[...] = jnp.zeros_like(total)
    lhs_b[...] = jnp.zeros_like(lhs_b)

    per_group = GROUP_W // CHUNK

    def two_chunks(i, carry):
        first = i * 2
        weigh(first, lhs_a)
        transform(lax.max(first - 1, 0), lhs_b)
        weigh(first + 1, lhs_b)
        transform(first, lhs_a)
        return carry

    for group in range(GROUPS):
        wait_group(group)
        lax.fori_loop(group * per_group // 2, (group + 1) * per_group // 2, two_chunks, 0)
    transform(N_CHUNK - 1, lhs_b)

    is_real = (lax.broadcasted_iota(jnp.int32, (EL, LANES), 1) & 8) == 0
    y = []
    for t in range(NSPEC):
        re = total[t * EL : (t + 1) * EL, :]
        im = total[(NSPEC + t) * EL : (NSPEC + t + 1) * EL, :]
        swapped = jnp.where(is_real, -pltpu.roll(im, LANES - 8, 1), pltpu.roll(im, 8, 1))
        y.append(re + swapped)
    place = lax.broadcasted_iota(jnp.int32, (EL, LANES), 1) >> 4
    for g in range(BANDS):
        for tile in range(2):
            out = jnp.zeros((EL, LANES), F32)
            for t in range(tile * 8, min(tile * 8 + 8, NSPEC)):
                moved = y[t]
                shift = (t - g) * 16 % LANES
                if shift:
                    moved = pltpu.roll(moved, shift, 1)
                out = jnp.where(place == t - tile * 8, moved, out)
            z[g, :, tile * LANES : (tile + 1) * LANES] = out.astype(BF16)
    share(
        n_band, n_blk, z, x, held, ct_send, ct_recv, ag_send, ag_recv, fw_send, fw_recv, here
    )


def places(n_band, n_blk):
    g, b = lax.axis_index("band"), lax.axis_index("blk")
    core, near, along = b % 2, b // 2 % 2, b // 4
    n_along = n_blk // 4

    def chip(d_along, d_near):
        return ((along + d_along + n_along) % n_along * 2 + (near + d_near) % 2) * 2 + core

    return g, b, b + 1 - 2 * core, chip


STEPS = ((1, 0), (-1, 0), (0, 1), (1, 1), (-1, 1))
PASSED = ((0, 0, 0), (1, 1, 1), (3, 0, 0), (4, 1, 1))


def greet(n_band, n_blk):
    g, b, sibling, chip = places(n_band, n_blk)
    peers = [((g + d) % n_band, b) for d in range(1, n_band)]
    peers += [(g, chip(*step)) for step in STEPS] + [(g, sibling)]
    barrier = pltpu.get_barrier_semaphore()
    for peer in peers:
        pl.semaphore_signal(barrier, inc=1, device_id=peer, device_id_type=MESH)


def share(n_band, n_blk, z, x, held, ct_send, ct_recv, ag_send, ag_recv, fw_send, fw_recv, here):
    g, b, sibling, chip = places(n_band, n_blk)
    pl.semaphore_wait(pltpu.get_barrier_semaphore(), n_band - 1 + len(STEPS) + 1)
    block = EL * n_band
    half = block // 2

    def rows(owner, part=None):
        if part is None:
            return pl.ds(pl.multiple_of(owner * block, block), block)
        return pl.ds(pl.multiple_of(owner * block + part * half, half), half)

    def remote(src, dst, send, recv, to):
        copy = pltpu.make_async_remote_copy(src, dst, send, recv, to, MESH)
        copy.start()
        return copy

    mine = pl.ds(pl.multiple_of(b * block + g * EL, EL), EL)
    turns = []
    for d in range(1, n_band):
        to = (g + d) % n_band
        turns.append(remote(z.at[to], held.at[mine], ct_send.at[d], ct_recv.at[d], (to, b)))
    keep = pltpu.make_async_copy(z.at[g], held.at[mine], here.at[0])
    keep.start()
    keep.wait()
    for turn in turns:
        turn.wait()

    me = rows(b)
    sends = [
        remote(held.at[me], held.at[me], ag_send.at[n], ag_recv.at[n], (g, chip(*step)))
        for n, step in enumerate(STEPS)
    ]
    passed, kept = [], []

    def hand_over(at, n):
        passed.append(remote(held.at[at], x.at[at], fw_send.at[n], fw_recv.at[n], (g, sibling)))
        kept.append(pltpu.make_async_copy(held.at[at], x.at[at], here.at[1 + n]))
        kept[-1].start()

    n_steps = len(STEPS)
    hand_over(me, 0)
    onward = [None] * len(PASSED)
    for n, (da, dn) in enumerate(STEPS):
        sends[n].wait_recv()
        owner = chip(-da, dn)
        for m, (brought, taken, part) in enumerate(PASSED):
            if brought == n:
                piece = held.at[rows(owner, part)]
                onward[m] = remote(
                    piece, piece, ag_send.at[n_steps + m], ag_recv.at[n_steps + m],
                    (g, chip(*STEPS[taken])),
                )
        hand_over(rows(owner), 1 + n)
    for m, (brought, taken, part) in enumerate(PASSED):
        onward[m].wait_recv()
        da = STEPS[brought][0] + STEPS[taken][0]
        hand_over(rows(chip(-da, STEPS[brought][1]), part), 1 + n_steps + m)
    for copy in kept:
        copy.wait()
    for copy in sends + onward:
        copy.wait_send()
    for copy in passed:
        copy.wait()


def front(volt, chans, n_band, n_blk):
    hbm = pl.BlockSpec(memory_space=pltpu.HBM)
    dma = pltpu.SemaphoreType.DMA
    everyone = EL * n_band * n_blk
    n_copies = len(STEPS) + len(PASSED)

    def body(*refs):
        front_kernel(n_band, n_blk, *refs)

    return pl.pallas_call(
        body,
        out_shape=jax.ShapeDtypeStruct((everyone, 2 * LANES), BF16),
        in_specs=[hbm] * 3,
        out_specs=hbm,
        scratch_shapes=[
            pltpu.SMEM((BANDS, SLOTS), jnp.int32),
            pltpu.VMEM((TAPS, C), F32),
            dma((2,)),
            pltpu.VMEM((GROUPS, FRAMES, 2, EL, GROUP_W), BF16),
            pltpu.VMEM((LANES, LANES), F32),
            pltpu.VMEM((LANES, LANES), F32),
            pltpu.VMEM((C // LANES, LANES), F32),
            pltpu.VMEM((C // LANES, LANES), F32),
            pltpu.VMEM((N_CHUNK, CHUNK, 2 * LANES), BF16),
            pltpu.VMEM((2 * ROWS, CHUNK), BF16),
            pltpu.VMEM((2 * ROWS, CHUNK), BF16),
            pltpu.VMEM((ROWS, LANES), F32),
            dma((GROUPS,)),
            pltpu.VMEM((BANDS, EL, 2 * LANES), BF16),
            pltpu.VMEM((everyone, 2 * LANES), BF16),
            dma((n_band,)),
            dma((n_band,)),
            dma((n_copies,)),
            dma((n_copies,)),
            dma((n_copies + 1,)),
            dma((n_copies + 1,)),
            dma((n_copies + 2,)),
        ],
        compiler_params=pltpu.CompilerParams(
            vmem_limit_bytes=48 * 2**20, collective_id=0, has_side_effects=True
        ),
        name="spectra",
    )(volt, chans, jnp.asarray(taper_table()))


COLUMNS = 512


def correlate_kernel(x_hbm, count, out, lhs, x, sems):
    j = pl.program_id(0)
    block = out.shape[3]
    b = lax.axis_index("blk")

    def fetch(step):
        at = pl.ds(pl.multiple_of(step * COLUMNS, COLUMNS), COLUMNS)
        return pltpu.make_async_copy(x_hbm.at[at], x.at[at], sems.at[step])

    mine = pl.ds(pl.multiple_of(b * block, block), block)
    own_ref = x.at[pl.ds(x_hbm.shape[0], block)]

    @pl.when(j == 0)
    def _():
        first = pltpu.make_async_copy(x_hbm.at[mine], own_ref, sems.at[pl.num_programs(0)])
        first.start()
        for step in range(x_hbm.shape[0] // COLUMNS):
            fetch(step).start()
        first.wait()
        live = count[lax.axis_index("band")]
        lane = lax.broadcasted_iota(jnp.int32, (block, LANES), 1)
        slot = lane & 7
        is_real = (lane & 8) == 0
        for tile in range(2):
            cols = slice(tile * LANES, (tile + 1) * LANES)
            own = own_ref[:, cols].astype(F32)
            turned = jnp.where(
                is_real, pltpu.roll(own, LANES - 8, 1), -pltpu.roll(own, 8, 1)
            )
            own = jnp.where(slot < live, own, 0.0)
            turned = jnp.where(slot < live, turned, 0.0)
            if tile == 1:
                used = lane < (NSPEC - 8) * 16
                own, turned = jnp.where(used, own, 0.0), jnp.where(used, turned, 0.0)
            for s in range(SLOTS):
                for part, value in ((0, own), (1, turned)):
                    at = (part * SLOTS + s) * block
                    lhs[at : at + block, cols] = jnp.where(slot == s, value, 0.0).astype(BF16)

    fetch(j).wait()
    right = x[pl.ds(pl.multiple_of(j * COLUMNS, COLUMNS), COLUMNS), :]
    y = lax.dot_general(
        lhs[...], right, (((1,), (1,)), ((), ())), preferred_element_type=F32
    )
    y = (y * (1.0 / NSPEC)).astype(BF16)
    for part in range(2):
        for s in range(SLOTS):
            at = (part * SLOTS + s) * block
            out[part, 0, s] = y[at : at + block]


def correlate(x, count, n_band, n_blk):
    everyone = x.shape[0]
    block = everyone // n_blk
    return pl.pallas_call(
        correlate_kernel,
        grid=(everyone // COLUMNS,),
        out_shape=jax.ShapeDtypeStruct((2, 1, SLOTS, block, everyone), BF16),
        in_specs=[
            pl.BlockSpec(memory_space=pltpu.HBM),
            pl.BlockSpec(memory_space=pltpu.SMEM),
        ],
        out_specs=pl.BlockSpec((2, 1, SLOTS, block, COLUMNS), lambda j: (0, 0, 0, 0, j)),
        scratch_shapes=[
            pltpu.VMEM((2 * SLOTS * block, x.shape[1]), BF16),
            pltpu.VMEM((everyone + block, x.shape[1]), BF16),
            pltpu.SemaphoreType.DMA((everyone // COLUMNS + 1,)),
        ],
        compiler_params=pltpu.CompilerParams(vmem_limit_bytes=32 * 2**20),
        name="correlate",
    )(x, count)


def solution(mesh):
    n_band, n_blk = mesh.shape["band"], mesh.shape["blk"]

    def local(volt, band_chans, band_count):
        x = front(volt, band_chans, n_band, n_blk)
        return correlate(x, band_count, n_band, n_blk)

    return jax.shard_map(
        local,
        mesh=mesh,
        in_specs=(P(None, ("blk", "band"), None), P(), P()),
        out_specs=P(None, "band", None, "blk", None),
        check_vma=False,
    )
```

time: 49.1 us -> 38.2 us (0.78)
  Pallas kernels: 45.3 us -> 36.4 us
  local copies, waits for them, and re-layouts: 3.48 us -> 1.64 us
    pallas_call x2 -> x1, Pallas kernels: 36.6 us -> 30.5 us  [front(): pl.pallas_call(body, out_shape=jax.ShapeDtypeStruct((everyone, 2 * LANES)...]
    pallas_call x1, Pallas kernels: 8.67 us -> 5.89 us  [correlate(): pl.pallas_call(correlate_kernel, grid=(everyone // COLUMNS,), out_shape=j...]
    unnamed x10 -> x6, local copies, waits for them, and re-layouts: 3.48 us -> 1.64 us
where the time goes in v1:
time: 38.2 us; the launch traced here: 38.1 us
  Pallas kernels  36.4 us (95%)
  local copies, waits for them, and re-layouts  1.64 us (4%)
    pallas_call x1, Pallas kernels, front(): pl.pallas_call(body, out_shape=jax.ShapeDtypeStruct((everyone, 2 * LANES)...  30.5 us
    pallas_call x1, Pallas kernels, correlate(): pl.pallas_call(correlate_kernel, grid=(everyone // COLUMNS,), out_shape=j...  5.89 us
    unnamed x6, local copies, waits for them, and re-layouts  1.64 us

profile of v1, /device:TPU:1, one launch (start us, length us, event | category | flops | bytes accessed | tf_op | source)
XLA Modules:
  0.0 38.1 jit_solution(5768363158098272385)
XLA Ops:
  0.0 0.0 copy-start
  0.0 0.9 %copy-done = f32[16,4096]{1,0:T(8,128)S(1)} copy-done((f32[16,4096]{1,0:T(8,128)S(1)}, f32[16,4096]{1,0:T(8,128)}, u32[]{:S(2)}) %copy-start) | copy-done | bytes 262168
  1.0 0.0 copy-start.1
  1.0 0.7 %copy-done.1 = s32[8,8]{1,0:T(8,128)S(1)} copy-done((s32[8,8]{1,0:T(8,128)S(1)}, s32[8,8]{1,0:T(8,128)}, u32[]{:S(2)}) %copy-start.1) | copy-done | bytes 280
  1.6 0.0 copy-start.2
  1.6 30.5 %spectra.1.x_hbm = bf16[2048,256]{1,0:T(8,128)(2,1)S(1)} custom-call(bf16[2,16,110592]{2,1,0:T(8,128)(2,1)} %refs_0_.1, s32[8,8]{1,0:T(8,128)S(1)} %copy-done.1, f32[16,4096]{1,0:T(8,128)S(1)} %copy-done), custom_call_target="tpu_custom_call" | custom-call | tf_op jit(solution)/shard_map/spectra/pallas_call | solution.py:292
  32.2 0.0 copy-done.2
  32.2 5.9 %correlate.1 = bf16[2,1,8,128,2048]{4,3,2,1,0:T(8,128)(2,1)} custom-call(bf16[2048,256]{1,0:T(8,128)(2,1)S(1)} %spectra.1.x_hbm, s32[8]{0:T(128)S(1)} %copy-done.2), custom_call_target="tpu_custom_call" | custom-call | tf_op jit(solution)/shard_map/correlate/pallas_call | solution.py:385
Async XLA Ops:
  0.0 0.9 %copy-start = (f32[16,4096]{1,0:T(8,128)S(1)}, f32[16,4096]{1,0:T(8,128)}, u32[]{:S(2)}) copy-start(f32[16,4096]{1,0:T(8,128)} %constant.2.clone.refs_2_) | copy-start | bytes 786436
  1.0 0.7 %copy-start.1 = (s32[8,8]{1,0:T(8,128)S(1)}, s32[8,8]{1,0:T(8,128)}, u32[]{:S(2)}) copy-start(s32[8,8]{1,0:T(8,128)} %refs_1_.1) | copy-start | bytes 772
  1.6 30.5 %copy-start.2 = (s32[8]{0:T(128)S(1)}, s32[8]{0:T(128)}, u32[]{:S(2)}) copy-start(s32[8]{0:T(128)} %count.1) | copy-start | bytes 100

commit v2 on v1

v2 whole, which is shorter than its diff:
```python
import math

import jax
import jax.numpy as jnp
import numpy as np
from jax import lax
from jax.experimental import pallas as pl
from jax.experimental.pallas import tpu as pltpu
from jax.sharding import PartitionSpec as P

C = 4096
TAPS = 16
NSPEC = 12
FRAMES = NSPEC + TAPS - 1
EL = 16
LANES = 128
BANDS = 8
SLOTS = 8
GROUPS = 4
GROUP_W = C // GROUPS
CHUNK = 512
N_CENTRE = 4
N_CHUNK = C // CHUNK
MESH = pl.DeviceIdType.MESH
F32, BF16 = jnp.float32, jnp.bfloat16


def taper_table():
    idx = np.arange(TAPS * C, dtype=np.float64)
    centre = (idx + 0.5) / C - TAPS / 2.0
    window = 0.5 - 0.5 * np.cos(2.0 * math.pi * (idx + 0.5) / (TAPS * C))
    prototype = np.sinc(centre) * window
    prototype = prototype / np.sqrt(np.sum(prototype * prototype))
    return prototype.reshape(TAPS, C).astype(np.float32)


def cos_sin(turns):
    shifted = turns + 512
    quarter = (shifted >> 10) & 3
    x = ((shifted & 1023) - 512).astype(F32) * (2.0 * math.pi / 4096.0)
    x2 = x * x
    s = x * (1.0 + x2 * (-1.0 / 6 + x2 * (1.0 / 120 + x2 * (-1.0 / 5040 + x2 * (1.0 / 362880)))))
    c = 1.0 + x2 * (-0.5 + x2 * (1.0 / 24 + x2 * (-1.0 / 720 + x2 * (1.0 / 40320))))
    odd = (quarter & 1) == 1
    cc, ss = jnp.where(odd, s, c), jnp.where(odd, c, s)
    cc = jnp.where((quarter == 1) | (quarter == 2), -cc, cc)
    ss = jnp.where(quarter >= 2, -ss, ss)
    return cc, ss


def split(y):
    hi = y.astype(BF16)
    return hi, (y - hi.astype(F32)).astype(BF16)


CENTRE = tuple(range(TAPS // 2 - N_CENTRE // 2, TAPS // 2 + N_CENTRE // 2))
OUTER = tuple(p for p in range(TAPS) if p not in CENTRE)
EARLY, LATE = range(8), range(8, NSPEC)


def front_kernel(
    n_band, n_blk, volt, chans_hbm, taper_hbm, x0, x1, chans, taper, small_sems, samples, base_c,
    base_s, step_c, step_s, table, lhs_a, lhs_b, total, sems, z0, z1, turned, held0, held1, *comm_sems
):
    greet(n_band, n_blk)
    def fetch(group, frame):
        return pltpu.make_async_copy(
            volt.at[:, :, pl.ds(frame * C + group * GROUP_W, GROUP_W)],
            samples.at[group, frame],
            sems.at[group],
        )

    small = [
        pltpu.make_async_copy(chans_hbm, chans, small_sems.at[0]),
        pltpu.make_async_copy(taper_hbm, taper, small_sems.at[1]),
    ]
    for copy in small:
        copy.start()
    for group in range(GROUPS):
        for frame in range(FRAMES):
            fetch(group, frame).start()
    small[0].wait()

    lane = lax.broadcasted_iota(jnp.int32, (8, LANES), 1)
    key = ((lane >> 4) << 3) + (lane & 7)
    row = jnp.zeros((8, LANES), jnp.int32)
    for g in range(BANDS):
        for s in range(SLOTS):
            row = jnp.where(key == g * SLOTS + s, chans[g, s], row)
    quarter_turn = ((lane[:1] >> 3) & 1) * 1024
    row = row[:1]
    inner = lax.broadcasted_iota(jnp.int32, (LANES, LANES), 0)
    c0, s0 = cos_sin((inner * row + quarter_turn) & 4095)
    base_c[...] = c0
    base_s[...] = s0
    outer = lax.broadcasted_iota(jnp.int32, (C // LANES, LANES), 0) * LANES
    c1, s1 = cos_sin((outer * row) & 4095)
    step_c[...] = c1
    step_s[...] = s1

    def build(chunk, carry):
        for part in range(CHUNK // LANES):
            a = chunk * (CHUNK // LANES) + part
            ca, sa = step_c[pl.ds(a, 1), :], step_s[pl.ds(a, 1), :]
            hi, lo = split(ca * base_c[...] - sa * base_s[...])
            rows = slice(part * LANES, (part + 1) * LANES)
            table[chunk, rows, :LANES] = hi
            table[chunk, rows, LANES:] = lo
        return carry

    lax.fori_loop(0, N_CHUNK, build, 0)

    def weigh(chunk, lhs, ts):
        rows = 2 * len(ts) * EL
        group = chunk // (GROUP_W // CHUNK)
        for part in range(CHUNK // LANES):
            k = pl.multiple_of(chunk * CHUNK + part * LANES, LANES)
            in_group = pl.multiple_of(k - group * GROUP_W, LANES)
            taps = [
                jnp.broadcast_to(taper[p : p + 1, pl.ds(k, LANES)], (EL, LANES))
                for p in range(TAPS)
            ]
            taps = [taps[p] if p in CENTRE else taps[p].astype(BF16) for p in range(TAPS)]
            column = slice(part * LANES, (part + 1) * LANES)
            for comp in range(2):
                side, mid = [None] * NSPEC, [None] * NSPEC
                for f in range(ts[0], ts[-1] + TAPS):
                    x = samples[group, f, comp, :, pl.ds(in_group, LANES)]
                    wide = x.astype(F32)
                    for t in range(max(ts[0], f - TAPS + 1), min(ts[-1], f) + 1):
                        p = f - t
                        if p in CENTRE:
                            term = taps[p] * wide
                            mid[t] = term if mid[t] is None else mid[t] + term
                        else:
                            term = taps[p] * x
                            side[t] = term if side[t] is None else side[t] + term
                    if f >= ts[0] + TAPS - 1:
                        t = f - TAPS + 1
                        hi, lo = split(mid[t] + side[t].astype(F32))
                        at = (comp * len(ts) + t - ts[0]) * EL
                        lhs[at : at + EL, column] = hi
                        lhs[rows + at : rows + at + EL, column] = lo

    def transform(chunk, lhs, ts):
        rows = 2 * len(ts) * EL
        at = 2 * ts[0] * EL
        r = jnp.dot(lhs[: 2 * rows, :], table[chunk], preferred_element_type=F32)
        total[at : at + rows, :] += (r[:rows, LANES:] + r[rows:, :LANES]) + r[:rows, :LANES]

    def wait_group(group):
        pltpu.make_async_copy(samples.at[group], samples.at[group], sems.at[group]).wait()

    small[1].wait()
    total[...] = jnp.zeros_like(total)
    per_group = GROUP_W // CHUNK

    def spectra_of(ts, first_pass):
        lhs_b[...] = jnp.zeros_like(lhs_b)

        def two_chunks(i, carry):
            first = i * 2
            weigh(first, lhs_a, ts)
            transform(lax.max(first - 1, 0), lhs_b, ts)
            weigh(first + 1, lhs_b, ts)
            transform(first, lhs_a, ts)
            return carry

        if first_pass:
            for group in range(GROUPS):
                wait_group(group)
                lax.fori_loop(
                    group * per_group // 2, (group + 1) * per_group // 2, two_chunks, 0
                )
        else:
            lax.fori_loop(0, N_CHUNK // 2, two_chunks, 0)
        transform(N_CHUNK - 1, lhs_b, ts)

    is_real = (lax.broadcasted_iota(jnp.int32, (EL, LANES), 1) & 8) == 0
    place = lax.broadcasted_iota(jnp.int32, (EL, LANES), 1) >> 4

    def by_band(ts, z):
        y = []
        for n in range(len(ts)):
            at = (2 * ts[0] + n) * EL
            re = total[at : at + EL, :]
            im = total[at + len(ts) * EL : at + (len(ts) + 1) * EL, :]
            swapped = jnp.where(is_real, -pltpu.roll(im, LANES - 8, 1), pltpu.roll(im, 8, 1))
            y.append(re + swapped)
        for g in range(BANDS):
            out = jnp.zeros((EL, LANES), F32)
            for n in range(len(ts)):
                shift = (n - g) * 16 % LANES
                moved = pltpu.roll(y[n], shift, 1) if shift else y[n]
                out = jnp.where(place == n, moved, out)
            z[g] = out.astype(BF16)

    early, late = Exchange(n_band, n_blk, 0, comm_sems), Exchange(n_band, n_blk, 1, comm_sems)
    spectra_of(EARLY, True)
    by_band(EARLY, z0)
    pl.semaphore_wait(pltpu.get_barrier_semaphore(), n_band - 1 + len(STEPS) + 1)
    block = EL * n_band
    mine = pl.ds(pl.multiple_of(lax.axis_index("blk") * block, block), block)
    early.turn(z0, held0.at[mine])
    spectra_of(LATE, False)
    by_band(LATE, z1)
    late.turn(z1, turned)
    early.turn_done()
    early.spread(held0, x0, block)
    early.pass_on()
    late.turn_done()
    half = block // 2
    top, bottom = turned[:half].astype(F32), turned[half:].astype(F32)
    packed = jnp.where(place[:1] < len(LATE), top, pltpu.roll(bottom, LANES // 2, 1)).astype(BF16)
    held1[pl.ds(pl.multiple_of(lax.axis_index("blk") * half, half), half), :] = packed
    late.spread(held1, x1, half)
    early.arrive()
    late.pass_on()
    late.arrive()
    early.finish()
    late.finish()


def places(n_band, n_blk):
    g, b = lax.axis_index("band"), lax.axis_index("blk")
    core, near, along = b % 2, b // 2 % 2, b // 4
    n_along = n_blk // 4

    def chip(d_along, d_near):
        return ((along + d_along + n_along) % n_along * 2 + (near + d_near) % 2) * 2 + core

    return g, b, b + 1 - 2 * core, chip


STEPS = ((1, 0), (-1, 0), (0, 1), (1, 1), (-1, 1))
PASSED = ((0, 0, 0), (1, 1, 1), (3, 0, 0), (4, 1, 1))


def greet(n_band, n_blk):
    g, b, sibling, chip = places(n_band, n_blk)
    peers = [((g + d) % n_band, b) for d in range(1, n_band)]
    peers += [(g, chip(*step)) for step in STEPS] + [(g, sibling)]
    barrier = pltpu.get_barrier_semaphore()
    for peer in peers:
        pl.semaphore_signal(barrier, inc=1, device_id=peer, device_id_type=MESH)


class Exchange:
    def __init__(self, n_band, n_blk, tile, sems):
        self.n_band = n_band
        self.g, self.b, self.sibling, self.chip = places(n_band, n_blk)
        self.sems = [sem.at[tile] for sem in sems]
        self.sends, self.onward, self.passed, self.kept = [], [], [], []

    def remote(self, src, dst, send, recv, to):
        copy = pltpu.make_async_remote_copy(src, dst, send, recv, to, MESH)
        copy.start()
        return copy

    def turn(self, z, block):
        g, send, recv, here = self.g, self.sems[0], self.sems[1], self.sems[6]
        mine = pl.ds(pl.multiple_of(g * EL, EL), EL)
        self.turns = []
        for d in range(1, self.n_band):
            to = (g + d) % self.n_band
            self.turns.append(
                self.remote(z.at[to], block.at[mine], send.at[d], recv.at[d], (to, self.b))
            )
        self.turns.append(pltpu.make_async_copy(z.at[g], block.at[mine], here.at[0]))
        self.turns[-1].start()

    def turn_done(self):
        for turn in self.turns:
            turn.wait()

    def rows(self, owner, part=None):
        if part is None:
            return pl.ds(pl.multiple_of(owner * self.block, self.block), self.block)
        half = self.block // 2
        return pl.ds(pl.multiple_of(owner * self.block + part * half, half), half)

    def hand_over(self, at, n):
        held, x, here = self.held, self.x, self.sems[6]
        self.passed.append(
            self.remote(
                held.at[at], x.at[at], self.sems[4].at[n], self.sems[5].at[n], (self.g, self.sibling)
            )
        )
        self.kept.append(pltpu.make_async_copy(held.at[at], x.at[at], here.at[1 + n]))
        self.kept[-1].start()

    def spread(self, held, x, block):
        self.held, self.x, self.block = held, x, block
        me = held.at[self.rows(self.b)]
        for n, step in enumerate(STEPS):
            self.sends.append(
                self.remote(
                    me, me, self.sems[2].at[n], self.sems[3].at[n], (self.g, self.chip(*step))
                )
            )
        self.hand_over(self.rows(self.b), 0)

    def pass_on(self):
        self.onward = [None] * len(PASSED)
        for n, (da, dn) in enumerate(STEPS):
            self.sends[n].wait_recv()
            owner = self.chip(-da, dn)
            for m, (brought, taken, part) in enumerate(PASSED):
                if brought == n:
                    piece = self.held.at[self.rows(owner, part)]
                    at = len(STEPS) + m
                    to = (self.g, self.chip(*STEPS[taken]))
                    self.onward[m] = self.remote(
                        piece, piece, self.sems[2].at[at], self.sems[3].at[at], to
                    )
            self.hand_over(self.rows(owner), 1 + n)

    def arrive(self):
        for m, (brought, taken, part) in enumerate(PASSED):
            self.onward[m].wait_recv()
            da = STEPS[brought][0] + STEPS[taken][0]
            owner = self.chip(-da, STEPS[brought][1])
            self.hand_over(self.rows(owner, part), 1 + len(STEPS) + m)

    def finish(self):
        for copy in self.kept:
            copy.wait()
        for copy in self.sends + self.onward:
            copy.wait_send()
        for copy in self.passed:
            copy.wait()


def front(volt, chans, n_band, n_blk):
    hbm = pl.BlockSpec(memory_space=pltpu.HBM)
    dma = pltpu.SemaphoreType.DMA
    everyone = EL * n_band * n_blk
    n_copies = len(STEPS) + len(PASSED)

    def body(*refs):
        front_kernel(n_band, n_blk, *refs)

    return pl.pallas_call(
        body,
        out_shape=[
            jax.ShapeDtypeStruct((everyone, LANES), BF16),
            jax.ShapeDtypeStruct((everyone // 2, LANES), BF16),
        ],
        in_specs=[hbm] * 3,
        out_specs=[hbm] * 2,
        scratch_shapes=[
            pltpu.SMEM((BANDS, SLOTS), jnp.int32),
            pltpu.VMEM((TAPS, C), F32),
            dma((2,)),
            pltpu.VMEM((GROUPS, FRAMES, 2, EL, GROUP_W), BF16),
            pltpu.VMEM((LANES, LANES), F32),
            pltpu.VMEM((LANES, LANES), F32),
            pltpu.VMEM((C // LANES, LANES), F32),
            pltpu.VMEM((C // LANES, LANES), F32),
            pltpu.VMEM((N_CHUNK, CHUNK, 2 * LANES), BF16),
            pltpu.VMEM((4 * len(EARLY) * EL, CHUNK), BF16),
            pltpu.VMEM((4 * len(EARLY) * EL, CHUNK), BF16),
            pltpu.VMEM((2 * NSPEC * EL, LANES), F32),
            dma((GROUPS,)),
            pltpu.VMEM((BANDS, EL, LANES), BF16),
            pltpu.VMEM((BANDS, EL, LANES), BF16),
            pltpu.VMEM((EL * n_band, LANES), BF16),
            pltpu.VMEM((everyone, LANES), BF16),
            pltpu.VMEM((everyone // 2, LANES), BF16),
            dma((2, n_band)),
            dma((2, n_band)),
            dma((2, n_copies)),
            dma((2, n_copies)),
            dma((2, n_copies + 1)),
            dma((2, n_copies + 1)),
            dma((2, n_copies + 2)),
        ],
        compiler_params=pltpu.CompilerParams(
            vmem_limit_bytes=60 * 2**20, collective_id=0, has_side_effects=True
        ),
        name="spectra",
    )(volt, chans, jnp.asarray(taper_table()))


COLUMNS = 512


def correlate_kernel(x0_hbm, x1_hbm, count, out, lhs, right, x0, x1, sems):
    j = pl.program_id(0)
    steps = x0_hbm.shape[0] // COLUMNS
    block = out.shape[3]
    half = block // 2
    b = lax.axis_index("blk")
    low = lax.broadcasted_iota(jnp.int32, (half, LANES), 1) < LANES // 2

    def fetch(step):
        pairs = []
        for n, (hbm, x) in enumerate(((x0_hbm, x0), (x1_hbm, x1))):
            width = COLUMNS // (1 + n)
            at = pl.ds(pl.multiple_of(step * width, width), width)
            pairs.append(pltpu.make_async_copy(hbm.at[at], x.at[at], sems.at[n, step]))
        return pairs

    def whole(packed):
        packed = packed.astype(F32)
        return packed, pltpu.roll(packed, LANES // 2, 1)

    @pl.when(j == 0)
    def _():
        own = []
        for n, (hbm, x) in enumerate(((x0_hbm, x0), (x1_hbm, x1))):
            rows = block // (1 + n)
            to = x.at[pl.ds(hbm.shape[0], rows)]
            at = pl.ds(pl.multiple_of(b * rows, rows), rows)
            own.append(pltpu.make_async_copy(hbm.at[at], to, sems.at[n, steps]))
            own[-1].start()
        for step in range(steps):
            for copy in fetch(step):
                copy.start()
        for copy in own:
            copy.wait()
        live = count[lax.axis_index("band")]

        def fill(own, at, cols, used):
            lane = lax.broadcasted_iota(jnp.int32, own.shape, 1)
            slot = lane & 7
            turned = jnp.where(
                (lane & 8) == 0, pltpu.roll(own, LANES - 8, 1), -pltpu.roll(own, 8, 1)
            )
            keep = (slot < live) & (lane < used)
            own, turned = jnp.where(keep, own, 0.0), jnp.where(keep, turned, 0.0)
            for s in range(SLOTS):
                for part, value in ((0, own), (1, turned)):
                    to = (part * SLOTS + s) * block + at
                    lhs[to : to + own.shape[0], cols] = jnp.where(slot == s, value, 0.0).astype(BF16)

        fill(x0[pl.ds(x0_hbm.shape[0], block), :].astype(F32), 0, slice(0, LANES), LANES)
        for n, part in enumerate(whole(x1[pl.ds(x1_hbm.shape[0], half), :])):
            fill(part, n * half, slice(LANES, 2 * LANES), len(LATE) * 16)

    for copy in fetch(j):
        copy.wait()
    right[:, :LANES] = x0[pl.ds(pl.multiple_of(j * COLUMNS, COLUMNS), COLUMNS), :]
    for n in range(COLUMNS // block):
        at = pl.multiple_of(j * (COLUMNS // 2) + n * half, half)
        first, second = whole(x1[pl.ds(at, half), :])
        for m, part in enumerate((first, second)):
            part = jnp.where(low, part, 0.0).astype(BF16)
            right[n * block + m * half : n * block + (m + 1) * half, LANES:] = part
    y = lax.dot_general(
        lhs[...], right[...], (((1,), (1,)), ((), ())), preferred_element_type=F32
    )
    y = (y * (1.0 / NSPEC)).astype(BF16)
    for part in range(2):
        for s in range(SLOTS):
            at = (part * SLOTS + s) * block
            out[part, 0, s] = y[at : at + block]


def correlate(x0, x1, count, n_band, n_blk):
    everyone = x0.shape[0]
    block = everyone // n_blk
    hbm = pl.BlockSpec(memory_space=pltpu.HBM)
    return pl.pallas_call(
        correlate_kernel,
        grid=(everyone // COLUMNS,),
        out_shape=jax.ShapeDtypeStruct((2, 1, SLOTS, block, everyone), BF16),
        in_specs=[hbm, hbm, pl.BlockSpec(memory_space=pltpu.SMEM)],
        out_specs=pl.BlockSpec((2, 1, SLOTS, block, COLUMNS), lambda j: (0, 0, 0, 0, j)),
        scratch_shapes=[
            pltpu.VMEM((2 * SLOTS * block, 2 * LANES), BF16),
            pltpu.VMEM((COLUMNS, 2 * LANES), BF16),
            pltpu.VMEM((everyone + block, LANES), BF16),
            pltpu.VMEM(((everyone + block) // 2, LANES), BF16),
            pltpu.SemaphoreType.DMA((2, everyone // COLUMNS + 1)),
        ],
        compiler_params=pltpu.CompilerParams(vmem_limit_bytes=60 * 2**20),
        name="correlate",
    )(x0, x1, count)


def solution(mesh):
    n_band, n_blk = mesh.shape["band"], mesh.shape["blk"]

    def local(volt, band_chans, band_count):
        x0, x1 = front(volt, band_chans, n_band, n_blk)
        return correlate(x0, x1, band_count, n_band, n_blk)

    return jax.shard_map(
        local,
        mesh=mesh,
        in_specs=(P(None, ("blk", "band"), None), P(), P()),
        out_specs=P(None, "band", None, "blk", None),
        check_vma=False,
    )
```

time: 38.2 us -> 40.2 us (1.052)
  Pallas kernels: 36.4 us -> 40.1 us
  local copies, waits for them, and re-layouts: 1.64 us -> 0 us
    pallas_call x1, Pallas kernels: 30.5 us -> 33.2 us  [front(): pl.pallas_call(body, out_shape=[jax.ShapeDtypeStruct((everyone, LANES), B...]
    unnamed x6 -> x0, local copies, waits for them, and re-layouts: 1.64 us -> none
    pallas_call x1, Pallas kernels: 5.89 us -> 6.91 us  [correlate(): pl.pallas_call(correlate_kernel, grid=(everyone // COLUMNS,), out_shape=j...]
where the time goes in v2:
time: 40.2 us; the launch traced here: 40.1 us
  Pallas kernels  40.1 us (100%)
    pallas_call x1, Pallas kernels, front(): pl.pallas_call(body, out_shape=[jax.ShapeDtypeStruct((everyone, LANES), B...  33.2 us
    pallas_call x1, Pallas kernels, correlate(): pl.pallas_call(correlate_kernel, grid=(everyone // COLUMNS,), out_shape=j...  6.91 us

profile of v2, /device:TPU:1, one launch (start us, length us, event | category | flops | bytes accessed | tf_op | source)
XLA Modules:
  0.0 40.1 jit_solution(12121394828755251215)
XLA Ops:
  0.0 33.2 %spectra.1 = (bf16[2048,128]{1,0:T(8,128)(2,1)}, bf16[1024,128]{1,0:T(8,128)(2,1)}) custom-call(bf16[2,16,110592]{2,1,0:T(8,128)(2,1)} %refs_0_.1, s32[8,8]{1,0:T(8,128)} %refs_1_.1, f32[16,4096]{1,0:T(8,128)} %constant.2.clone.refs_2_), custom_call_target="tpu_custom_call" | custom-call | tf_op jit(solution)/shard_map/spectra/pallas_call | solution.py:343
  33.2 6.9 %correlate.1 = bf16[2,1,8,128,2048]{4,3,2,1,0:T(8,128)(2,1)} custom-call(bf16[2048,128]{1,0:T(8,128)(2,1)} %get-tuple-element.7.x0_hbm, bf16[1024,128]{1,0:T(8,128)(2,1)} %get-tuple-element.8.x1_hbm, s32[8]{0:T(128)} %count.1), custom_call_target="tpu_custom_call" | custom-call | tf_op jit(solution)/shard_map/correlate/pallas_call | solution.py:464

commit v3 on v1

--- a/solution.py
+++ b/solution.py
@@ -25,13 +25,36 @@
 F32, BF16 = jnp.float32, jnp.bfloat16
 
 
-def taper_table():
+def taper_scale():
     idx = np.arange(TAPS * C, dtype=np.float64)
     centre = (idx + 0.5) / C - TAPS / 2.0
     window = 0.5 - 0.5 * np.cos(2.0 * math.pi * (idx + 0.5) / (TAPS * C))
     prototype = np.sinc(centre) * window
-    prototype = prototype / np.sqrt(np.sum(prototype * prototype))
-    return prototype.reshape(TAPS, C).astype(np.float32)
+    return float(1.0 / np.sqrt(np.sum(prototype * prototype)))
+
+
+def half_sine(x):
+    y = jnp.minimum(x, math.pi - x)
+    y2 = y * y
+    s = 1.0 / 120 + y2 * (-1.0 / 5040 + y2 * (1.0 / 362880 + y2 * (-1.0 / 39916800)))
+    return y * (1.0 + y2 * (-1.0 / 6 + y2 * s))
+
+
+def fill_taper(taper):
+    width = 512
+    scale = taper_scale() / math.pi
+
+    def some(n, carry):
+        tap = lax.broadcasted_iota(jnp.int32, (TAPS, width), 0)
+        k = lax.broadcasted_iota(jnp.int32, (TAPS, width), 1) + n * width
+        frac = (k.astype(F32) + 0.5) * (1.0 / C)
+        top = half_sine(frac * math.pi) * jnp.where((tap & 1) == 0, scale, -scale)
+        window = half_sine((tap.astype(F32) + frac) * (math.pi / TAPS))
+        value = top * window * window / (frac + (tap - TAPS // 2).astype(F32))
+        taper[:, pl.ds(pl.multiple_of(n * width, width), width)] = value
+        return carry
+
+    lax.fori_loop(0, C // width, some, 0)
 
 
 def cos_sin(turns):
@@ -59,11 +82,10 @@
 
 
 def front_kernel(
-    n_band, n_blk, volt, chans_hbm, taper_hbm, x, chans, taper, small_sems, samples, base_c, base_s,
-    step_c, step_s, table, lhs_a, lhs_b, total, sems, z, held, ct_send, ct_recv, ag_send, ag_recv,
-    fw_send, fw_recv, here,
+    n_band, n_blk, volt, chans_hbm, x, chans, taper, small_sem, samples, base_c, base_s, step_c, step_s,
+    table, lhs_a, lhs_b, total, sems, z, turned, ct_send, ct_recv, ag_send, ag_recv, fw_send, fw_recv,
+    here,
 ):
-    greet(n_band, n_blk)
     def fetch(group, frame):
         return pltpu.make_async_copy(
             volt.at[:, :, pl.ds(frame * C + group * GROUP_W, GROUP_W)],
@@ -71,16 +93,17 @@
             sems.at[group],
         )
 
-    small = [
-        pltpu.make_async_copy(chans_hbm, chans, small_sems.at[0]),
-        pltpu.make_async_copy(taper_hbm, taper, small_sems.at[1]),
-    ]
-    for copy in small:
-        copy.start()
-    for group in range(GROUPS):
+    def fetch_group(group):
         for frame in range(FRAMES):
             fetch(group, frame).start()
-    small[0].wait()
+
+    small = pltpu.make_async_copy(chans_hbm, chans, small_sem.at[0])
+    small.start()
+    fetch_group(0)
+    greet(n_band, n_blk)
+    fetch_group(1)
+    fill_taper(taper)
+    small.wait()
 
     lane = lax.broadcasted_iota(jnp.int32, (8, LANES), 1)
     key = ((lane >> 4) << 3) + (lane & 7)
@@ -149,7 +172,6 @@
     def wait_group(group):
         pltpu.make_async_copy(samples.at[group], samples.at[group], sems.at[group]).wait()
 
-    small[1].wait()
     total[...] = jnp.zeros_like(total)
     lhs_b[...] = jnp.zeros_like(lhs_b)
 
@@ -164,6 +186,8 @@
         return carry
 
     for group in range(GROUPS):
+        if group + 2 < GROUPS:
+            fetch_group(group + 2)
         wait_group(group)
         lax.fori_loop(group * per_group // 2, (group + 1) * per_group // 2, two_chunks, 0)
     transform(N_CHUNK - 1, lhs_b)
@@ -187,7 +211,7 @@
                 out = jnp.where(place == t - tile * 8, moved, out)
             z[g, :, tile * LANES : (tile + 1) * LANES] = out.astype(BF16)
     share(
-        n_band, n_blk, z, x, held, ct_send, ct_recv, ag_send, ag_recv, fw_send, fw_recv, here
+        n_band, n_blk, z, turned, x, ct_send, ct_recv, ag_send, ag_recv, fw_send, fw_recv, here
     )
 
 
@@ -202,8 +226,15 @@
     return g, b, b + 1 - 2 * core, chip
 
 
-STEPS = ((1, 0), (-1, 0), (0, 1), (1, 1), (-1, 1))
-PASSED = ((0, 0, 0), (1, 1, 1), (3, 0, 0), (4, 1, 1))
+STEPS = ((1, 0), (-1, 1), (-1, 0), (1, 1), (0, 1))
+PASSED = (0, 1)
+
+
+def slot_of(d_along, d_near):
+    return {0: 0, 1: 2, 3: 4, 2: 6}[d_along % 4] + d_near
+
+
+PACKED = 192
 
 
 def greet(n_band, n_blk):
@@ -215,65 +246,54 @@
         pl.semaphore_signal(barrier, inc=1, device_id=peer, device_id_type=MESH)
 
 
-def share(n_band, n_blk, z, x, held, ct_send, ct_recv, ag_send, ag_recv, fw_send, fw_recv, here):
+def share(n_band, n_blk, z, turned, x, ct_send, ct_recv, ag_send, ag_recv, fw_send, fw_recv, here):
     g, b, sibling, chip = places(n_band, n_blk)
     pl.semaphore_wait(pltpu.get_barrier_semaphore(), n_band - 1 + len(STEPS) + 1)
-    block = EL * n_band
-    half = block // 2
-
-    def rows(owner, part=None):
-        if part is None:
-            return pl.ds(pl.multiple_of(owner * block, block), block)
-        return pl.ds(pl.multiple_of(owner * block + part * half, half), half)
+    half = EL * n_band // 2
+    first = b % 2 * (n_blk // 2)
+
+    def slots(start, count=1):
+        at = pl.multiple_of((first + start) * PACKED, PACKED)
+        return x.at[pl.ds(at, count * PACKED)]
 
     def remote(src, dst, send, recv, to):
         copy = pltpu.make_async_remote_copy(src, dst, send, recv, to, MESH)
         copy.start()
         return copy
 
-    mine = pl.ds(pl.multiple_of(b * block + g * EL, EL), EL)
+    mine = turned.at[pl.ds(pl.multiple_of(g * EL, EL), EL)]
     turns = []
     for d in range(1, n_band):
         to = (g + d) % n_band
-        turns.append(remote(z.at[to], held.at[mine], ct_send.at[d], ct_recv.at[d], (to, b)))
-    keep = pltpu.make_async_copy(z.at[g], held.at[mine], here.at[0])
-    keep.start()
-    keep.wait()
+        turns.append(remote(z.at[to], mine, ct_send.at[d], ct_recv.at[d], (to, b)))
+    turns.append(pltpu.make_async_copy(z.at[g], mine, here.at[0]))
+    turns[-1].start()
     for turn in turns:
         turn.wait()
-
-    me = rows(b)
+    own = slots(0)
+    low = lax.broadcasted_iota(jnp.int32, (half, LANES), 1) < LANES // 2
+    top = turned[:half, LANES:].astype(F32)
+    bottom = pltpu.roll(turned[half:, LANES:].astype(F32), LANES // 2, 1)
+    own[: 2 * half, :] = turned[:, :LANES]
+    own[2 * half :, :] = jnp.where(low, top, bottom).astype(BF16)
+
     sends = [
-        remote(held.at[me], held.at[me], ag_send.at[n], ag_recv.at[n], (g, chip(*step)))
-        for n, step in enumerate(STEPS)
+        remote(own, slots(slot_of(-da, dn)), ag_send.at[n], ag_recv.at[n], (g, chip(da, dn)))
+        for n, (da, dn) in enumerate(STEPS)
     ]
-    passed, kept = [], []
-
-    def hand_over(at, n):
-        passed.append(remote(held.at[at], x.at[at], fw_send.at[n], fw_recv.at[n], (g, sibling)))
-        kept.append(pltpu.make_async_copy(held.at[at], x.at[at], here.at[1 + n]))
-        kept[-1].start()
-
-    n_steps = len(STEPS)
-    hand_over(me, 0)
-    onward = [None] * len(PASSED)
+    onward = []
     for n, (da, dn) in enumerate(STEPS):
         sends[n].wait_recv()
-        owner = chip(-da, dn)
-        for m, (brought, taken, part) in enumerate(PASSED):
-            if brought == n:
-                piece = held.at[rows(owner, part)]
-                onward[m] = remote(
-                    piece, piece, ag_send.at[n_steps + m], ag_recv.at[n_steps + m],
-                    (g, chip(*STEPS[taken])),
-                )
-        hand_over(rows(owner), 1 + n)
-    for m, (brought, taken, part) in enumerate(PASSED):
-        onward[m].wait_recv()
-        da = STEPS[brought][0] + STEPS[taken][0]
-        hand_over(rows(chip(-da, STEPS[brought][1]), part), 1 + n_steps + m)
-    for copy in kept:
-        copy.wait()
+        if n in PASSED:
+            m = len(STEPS) + len(onward)
+            came, goes = slots(slot_of(-da, dn)), slots(slot_of(-2 * da, dn))
+            onward.append(remote(came, goes, ag_send.at[m], ag_recv.at[m], (g, chip(da, 0))))
+    near = slots(0, len(STEPS) + 1)
+    passed = [remote(near, near, fw_send.at[0], fw_recv.at[0], (g, sibling))]
+    for copy in onward:
+        copy.wait_recv()
+    far = slots(len(STEPS) + 1, 2)
+    passed.append(remote(far, far, fw_send.at[1], fw_recv.at[1], (g, sibling)))
     for copy in sends + onward:
         copy.wait_send()
     for copy in passed:
@@ -283,21 +303,21 @@
 def front(volt, chans, n_band, n_blk):
     hbm = pl.BlockSpec(memory_space=pltpu.HBM)
     dma = pltpu.SemaphoreType.DMA
-    everyone = EL * n_band * n_blk
     n_copies = len(STEPS) + len(PASSED)
+    vmem = pl.BlockSpec(memory_space=pltpu.VMEM)
 
     def body(*refs):
         front_kernel(n_band, n_blk, *refs)
 
     return pl.pallas_call(
         body,
-        out_shape=jax.ShapeDtypeStruct((everyone, 2 * LANES), BF16),
-        in_specs=[hbm] * 3,
-        out_specs=hbm,
+        out_shape=jax.ShapeDtypeStruct((n_blk * PACKED, LANES), BF16),
+        in_specs=[hbm] * 2,
+        out_specs=vmem,
         scratch_shapes=[
             pltpu.SMEM((BANDS, SLOTS), jnp.int32),
             pltpu.VMEM((TAPS, C), F32),
-            dma((2,)),
+            dma((1,)),
             pltpu.VMEM((GROUPS, FRAMES, 2, EL, GROUP_W), BF16),
             pltpu.VMEM((LANES, LANES), F32),
             pltpu.VMEM((LANES, LANES), F32),
@@ -309,68 +329,73 @@
             pltpu.VMEM((ROWS, LANES), F32),
             dma((GROUPS,)),
             pltpu.VMEM((BANDS, EL, 2 * LANES), BF16),
-            pltpu.VMEM((everyone, 2 * LANES), BF16),
+            pltpu.VMEM((EL * n_band, 2 * LANES), BF16),
             dma((n_band,)),
             dma((n_band,)),
             dma((n_copies,)),
             dma((n_copies,)),
-            dma((n_copies + 1,)),
-            dma((n_copies + 1,)),
-            dma((n_copies + 2,)),
+            dma((2,)),
+            dma((2,)),
+            dma((1,)),
         ],
         compiler_params=pltpu.CompilerParams(
             vmem_limit_bytes=48 * 2**20, collective_id=0, has_side_effects=True
         ),
         name="spectra",
-    )(volt, chans, jnp.asarray(taper_table()))
+    )(volt, chans)
 
 
 COLUMNS = 512
 
 
-def correlate_kernel(x_hbm, count, out, lhs, x, sems):
+def correlate_kernel(n_blk, x, count, out, lhs, right):
     j = pl.program_id(0)
     block = out.shape[3]
+    half = block // 2
     b = lax.axis_index("blk")
-
-    def fetch(step):
-        at = pl.ds(pl.multiple_of(step * COLUMNS, COLUMNS), COLUMNS)
-        return pltpu.make_async_copy(x_hbm.at[at], x.at[at], sems.at[step])
-
-    mine = pl.ds(pl.multiple_of(b * block, block), block)
-    own_ref = x.at[pl.ds(x_hbm.shape[0], block)]
+    near, along = b // 2 % 2, b // 4
+
+    def rows_of(owner):
+        d_near = (owner // 2 + near) % 2
+        d_along = (owner // 4 - along + n_blk // 4) % (n_blk // 4)
+        slot = jnp.where(d_along == 3, 4, jnp.where(d_along == 2, 6, 2 * d_along)) + d_near
+        return pl.multiple_of((owner % 2 * (n_blk // 2) + slot) * PACKED, PACKED)
+
+    def late_tile(at):
+        packed = x[pl.ds(at + block, half), :].astype(F32)
+        return packed, pltpu.roll(packed, LANES // 2, 1)
 
     @pl.when(j == 0)
     def _():
-        first = pltpu.make_async_copy(x_hbm.at[mine], own_ref, sems.at[pl.num_programs(0)])
-        first.start()
-        for step in range(x_hbm.shape[0] // COLUMNS):
-            fetch(step).start()
-        first.wait()
         live = count[lax.axis_index("band")]
-        lane = lax.broadcasted_iota(jnp.int32, (block, LANES), 1)
-        slot = lane & 7
-        is_real = (lane & 8) == 0
-        for tile in range(2):
-            cols = slice(tile * LANES, (tile + 1) * LANES)
-            own = own_ref[:, cols].astype(F32)
+
+        def fill(own, at, cols, used):
+            lane = lax.broadcasted_iota(jnp.int32, own.shape, 1)
+            slot = lane & 7
             turned = jnp.where(
-                is_real, pltpu.roll(own, LANES - 8, 1), -pltpu.roll(own, 8, 1)
+                (lane & 8) == 0, pltpu.roll(own, LANES - 8, 1), -pltpu.roll(own, 8, 1)
             )
-            own = jnp.where(slot < live, own, 0.0)
-            turned = jnp.where(slot < live, turned, 0.0)
-            if tile == 1:
-                used = lane < (NSPEC - 8) * 16
-                own, turned = jnp.where(used, own, 0.0), jnp.where(used, turned, 0.0)
+            keep = (slot < live) & (lane < used)
+            own, turned = jnp.where(keep, own, 0.0), jnp.where(keep, turned, 0.0)
             for s in range(SLOTS):
                 for part, value in ((0, own), (1, turned)):
-                    at = (part * SLOTS + s) * block
-                    lhs[at : at + block, cols] = jnp.where(slot == s, value, 0.0).astype(BF16)
-
-    fetch(j).wait()
-    right = x[pl.ds(pl.multiple_of(j * COLUMNS, COLUMNS), COLUMNS), :]
+                    to = (part * SLOTS + s) * block + at
+                    lhs[to : to + own.shape[0], cols] = jnp.where(slot == s, value, 0.0).astype(BF16)
+
+        mine = rows_of(b)
+        fill(x[pl.ds(mine, block), :].astype(F32), 0, slice(0, LANES), LANES)
+        for n, part in enumerate(late_tile(mine)):
+            fill(part, n * half, slice(LANES, 2 * LANES), (NSPEC - 8) * 16)
+
+    low = lax.broadcasted_iota(jnp.int32, (half, LANES), 1) < LANES // 2
+    for n in range(COLUMNS // block):
+        at = rows_of(j * (COLUMNS // block) + n)
+        right[n * block : (n + 1) * block, :LANES] = x[pl.ds(at, block), :]
+        for m, part in enumerate(late_tile(at)):
+            to = n * block + m * half
+            right[to : to + half, LANES:] = jnp.where(low, part, 0.0).astype(BF16)
     y = lax.dot_general(
-        lhs[...], right, (((1,), (1,)), ((), ())), preferred_element_type=F32
+        lhs[...], right[...], (((1,), (1,)), ((), ())), preferred_element_type=F32
     )
     y = (y * (1.0 / NSPEC)).astype(BF16)
     for part in range(2):
@@ -380,21 +405,24 @@
 
 
 def correlate(x, count, n_band, n_blk):
-    everyone = x.shape[0]
-    block = everyone // n_blk
+    block = EL * n_band
+    everyone = block * n_blk
+
+    def body(*refs):
+        correlate_kernel(n_blk, *refs)
+
     return pl.pallas_call(
-        correlate_kernel,
+        body,
         grid=(everyone // COLUMNS,),
         out_shape=jax.ShapeDtypeStruct((2, 1, SLOTS, block, everyone), BF16),
         in_specs=[
-            pl.BlockSpec(memory_space=pltpu.HBM),
+            pl.BlockSpec(memory_space=pltpu.VMEM),
             pl.BlockSpec(memory_space=pltpu.SMEM),
         ],
         out_specs=pl.BlockSpec((2, 1, SLOTS, block, COLUMNS), lambda j: (0, 0, 0, 0, j)),
         scratch_shapes=[
-            pltpu.VMEM((2 * SLOTS * block, x.shape[1]), BF16),
-            pltpu.VMEM((everyone + block, x.shape[1]), BF16),
-            pltpu.SemaphoreType.DMA((everyone // COLUMNS + 1,)),
+            pltpu.VMEM((2 * SLOTS * block, 2 * LANES), BF16),
+            pltpu.VMEM((COLUMNS, 2 * LANES), BF16),
         ],
         compiler_params=pltpu.CompilerParams(vmem_limit_bytes=32 * 2**20),
         name="correlate",

time: 38.2 us -> 36.4 us (0.953)
  Pallas kernels: 36.4 us -> 34.9 us
    pallas_call x2, Pallas kernels: 36.4 us -> 34.9 us  [the longest x1 28.8 us: front(): pl.pallas_call(body, out_shape=jax.ShapeDtypeStruct((n_blk * PACKED, LANE...]
    unnamed x6 -> x4, local copies, waits for them, and re-layouts: 1.64 us -> 1.34 us
where the time goes in v3:
time: 36.4 us; the launch traced here: 36.2 us
  Pallas kernels  34.9 us (96%)
  local copies, waits for them, and re-layouts  1.34 us (4%)
    pallas_call x1, Pallas kernels, front(): pl.pallas_call(body, out_shape=jax.ShapeDtypeStruct((n_blk * PACKED, LANE...  28.8 us
    pallas_call x1, Pallas kernels, correlate(): pl.pallas_call(body, grid=(everyone // COLUMNS,), out_shape=jax.ShapeDtyp...  6.05 us
    unnamed x4, local copies, waits for them, and re-layouts  1.34 us

profile of v3, /device:TPU:1, one launch (start us, length us, event | category | flops | bytes accessed | tf_op | source)
XLA Modules:
  0.0 36.2 jit_solution(11289445473618392563)
XLA Ops:
  0.0 0.0 copy-start
  0.0 0.7 %copy-done = s32[8,8]{1,0:T(8,128)S(1)} copy-done((s32[8,8]{1,0:T(8,128)S(1)}, s32[8,8]{1,0:T(8,128)}, u32[]{:S(2)}) %copy-start) | copy-done | bytes 280
  0.7 28.8 %spectra.1.refs_0_ = bf16[3072,128]{1,0:T(8,128)(2,1)S(1)} custom-call(bf16[2,16,110592]{2,1,0:T(8,128)(2,1)} %refs_0_.1, s32[8,8]{1,0:T(8,128)S(1)} %copy-done), custom_call_target="tpu_custom_call" | custom-call | tf_op jit(solution)/shard_map/spectra/pallas_call | solution.py:312
  29.5 0.0 copy-start.1
  29.5 0.6 %copy-done.1 = s32[8]{0:T(128)S(1)} copy-done((s32[8]{0:T(128)S(1)}, s32[8]{0:T(128)}, u32[]{:S(2)}) %copy-start.1) | copy-done | bytes 56
  30.2 6.0 %correlate.1 = bf16[2,1,8,128,2048]{4,3,2,1,0:T(8,128)(2,1)} custom-call(bf16[3072,128]{1,0:T(8,128)(2,1)S(1)} %spectra.1.refs_0_, s32[8]{0:T(128)S(1)} %copy-done.1), custom_call_target="tpu_custom_call" | custom-call | tf_op jit(solution)/shard_map/correlate/pallas_call | solution.py:414
Async XLA Ops:
  0.0 0.7 %copy-start = (s32[8,8]{1,0:T(8,128)S(1)}, s32[8,8]{1,0:T(8,128)}, u32[]{:S(2)}) copy-start(s32[8,8]{1,0:T(8,128)} %refs_1_.2) | copy-start | bytes 772
  29.5 0.7 %copy-start.1 = (s32[8]{0:T(128)S(1)}, s32[8]{0:T(128)}, u32[]{:S(2)}) copy-start(s32[8]{0:T(128)} %refs_1_.3) | copy-start | bytes 100

commit v4 on v3

--- a/solution.py
+++ b/solution.py
@@ -82,9 +82,8 @@
 
 
 def front_kernel(
-    n_band, n_blk, volt, chans_hbm, x, chans, taper, small_sem, samples, base_c, base_s, step_c, step_s,
-    table, lhs_a, lhs_b, total, sems, z, turned, ct_send, ct_recv, ag_send, ag_recv, fw_send, fw_recv,
-    here,
+    n_band, n_blk, volt, chans_hbm, left, right, chans, taper, small_sem, samples, base_c, base_s,
+    step_c, step_s, table, lhs_a, lhs_b, total, sems, z, turned, x, *comm_sems
 ):
     def fetch(group, frame):
         return pltpu.make_async_copy(
@@ -210,9 +209,7 @@
                     moved = pltpu.roll(moved, shift, 1)
                 out = jnp.where(place == t - tile * 8, moved, out)
             z[g, :, tile * LANES : (tile + 1) * LANES] = out.astype(BF16)
-    share(
-        n_band, n_blk, z, turned, x, ct_send, ct_recv, ag_send, ag_recv, fw_send, fw_recv, here
-    )
+    share(n_band, n_blk, z, turned, x, chans, left, right, *comm_sems)
 
 
 def places(n_band, n_blk):
@@ -230,8 +227,11 @@
 PASSED = (0, 1)
 
 
+NEARBY = ((0, 0), (0, 1), (1, 0), (1, 1), (-1, 0), (-1, 1), (2, 0), (2, 1))
+
+
 def slot_of(d_along, d_near):
-    return {0: 0, 1: 2, 3: 4, 2: 6}[d_along % 4] + d_near
+    return NEARBY.index(((d_along + 1) % 4 - 1, d_near))
 
 
 PACKED = 192
@@ -246,58 +246,97 @@
         pl.semaphore_signal(barrier, inc=1, device_id=peer, device_id_type=MESH)
 
 
-def share(n_band, n_blk, z, turned, x, ct_send, ct_recv, ag_send, ag_recv, fw_send, fw_recv, here):
+def fill_left(left, turned, live):
+    block = turned.shape[0]
+    for tile in range(2):
+        cols = slice(tile * LANES, (tile + 1) * LANES)
+        own = turned[:, cols].astype(F32)
+        lane = lax.broadcasted_iota(jnp.int32, own.shape, 1)
+        slot = lane & 7
+        crossed = jnp.where(
+            (lane & 8) == 0, pltpu.roll(own, LANES - 8, 1), -pltpu.roll(own, 8, 1)
+        )
+        own, crossed = jnp.where(slot < live, own, 0.0), jnp.where(slot < live, crossed, 0.0)
+        for s in range(SLOTS):
+            for part, value in ((0, own), (1, crossed)):
+                at = (part * SLOTS + s) * block
+                left[at : at + block, cols] = jnp.where(slot == s, value, 0.0).astype(BF16)
+
+
+def share(
+    n_band, n_blk, z, turned, x, chans, left, right, ct_send, ct_recv, ag_send, ag_recv, fw_send,
+    fw_recv, here,
+):
     g, b, sibling, chip = places(n_band, n_blk)
     pl.semaphore_wait(pltpu.get_barrier_semaphore(), n_band - 1 + len(STEPS) + 1)
-    half = EL * n_band // 2
-    first = b % 2 * (n_blk // 2)
-
-    def slots(start, count=1):
-        at = pl.multiple_of((first + start) * PACKED, PACKED)
+    block = EL * n_band
+    half = block // 2
+    core = b % 2
+    low = lax.broadcasted_iota(jnp.int32, (half, LANES), 1) < LANES // 2
+
+    def slots(of_core, start, count=1):
+        at = pl.multiple_of((of_core * (n_blk // 2) + start) * PACKED, PACKED)
         return x.at[pl.ds(at, count * PACKED)]
 
     def remote(src, dst, send, recv, to):
         copy = pltpu.make_async_remote_copy(src, dst, send, recv, to, MESH)
         copy.start()
         return copy
+
+    def unpack(of_core, first, count):
+        for slot in range(first, first + count):
+            owner = chip(*NEARBY[slot]) - core + of_core
+            at = pl.multiple_of(owner * block, block)
+            kept = slots(of_core, slot)
+            right[pl.ds(at, block), :LANES] = kept[:block, :]
+            packed = kept[block:, :].astype(F32)
+            for n, part in enumerate((packed, pltpu.roll(packed, LANES // 2, 1))):
+                part = jnp.where(low, part, 0.0).astype(BF16)
+                right[pl.ds(pl.multiple_of(at + n * half, half), half), LANES:] = part
 
     mine = turned.at[pl.ds(pl.multiple_of(g * EL, EL), EL)]
     turns = []
     for d in range(1, n_band):
         to = (g + d) % n_band
         turns.append(remote(z.at[to], mine, ct_send.at[d], ct_recv.at[d], (to, b)))
-    turns.append(pltpu.make_async_copy(z.at[g], mine, here.at[0]))
-    turns[-1].start()
+    keep = pltpu.make_async_copy(z.at[g], mine, here.at[0])
+    keep.start()
+    keep.wait()
     for turn in turns:
-        turn.wait()
-    own = slots(0)
-    low = lax.broadcasted_iota(jnp.int32, (half, LANES), 1) < LANES // 2
+        turn.wait_recv()
+    own = slots(core, 0)
     top = turned[:half, LANES:].astype(F32)
     bottom = pltpu.roll(turned[half:, LANES:].astype(F32), LANES // 2, 1)
-    own[: 2 * half, :] = turned[:, :LANES]
-    own[2 * half :, :] = jnp.where(low, top, bottom).astype(BF16)
+    own[:block, :] = turned[:, :LANES]
+    own[block:, :] = jnp.where(low, top, bottom).astype(BF16)
 
     sends = [
-        remote(own, slots(slot_of(-da, dn)), ag_send.at[n], ag_recv.at[n], (g, chip(da, dn)))
+        remote(own, slots(core, slot_of(-da, dn)), ag_send.at[n], ag_recv.at[n], (g, chip(da, dn)))
         for n, (da, dn) in enumerate(STEPS)
     ]
+    fill_left(left, turned, chans[BANDS, g])
+    unpack(core, 0, 1)
     onward = []
     for n, (da, dn) in enumerate(STEPS):
         sends[n].wait_recv()
         if n in PASSED:
             m = len(STEPS) + len(onward)
-            came, goes = slots(slot_of(-da, dn)), slots(slot_of(-2 * da, dn))
+            came, goes = slots(core, slot_of(-da, dn)), slots(core, slot_of(-2 * da, dn))
             onward.append(remote(came, goes, ag_send.at[m], ag_recv.at[m], (g, chip(da, 0))))
-    near = slots(0, len(STEPS) + 1)
-    passed = [remote(near, near, fw_send.at[0], fw_recv.at[0], (g, sibling))]
+    n_near = len(STEPS) + 1
+    near, far = slots(core, 0, n_near), slots(core, n_near, 2)
+    near_copy = remote(near, near, fw_send.at[0], fw_recv.at[0], (g, sibling))
+    unpack(core, 1, n_near - 1)
+    near_copy.wait_recv()
+    unpack(1 - core, 0, n_near)
     for copy in onward:
         copy.wait_recv()
-    far = slots(len(STEPS) + 1, 2)
-    passed.append(remote(far, far, fw_send.at[1], fw_recv.at[1], (g, sibling)))
-    for copy in sends + onward:
+    far_copy = remote(far, far, fw_send.at[1], fw_recv.at[1], (g, sibling))
+    unpack(core, n_near, 2)
+    far_copy.wait_recv()
+    unpack(1 - core, n_near, 2)
+    for copy in turns + sends + onward + [near_copy, far_copy]:
         copy.wait_send()
-    for copy in passed:
-        copy.wait()
 
 
 def front(volt, chans, n_band, n_blk):
@@ -311,11 +350,14 @@
 
     return pl.pallas_call(
         body,
-        out_shape=jax.ShapeDtypeStruct((n_blk * PACKED, LANES), BF16),
+        out_shape=[
+            jax.ShapeDtypeStruct((2 * SLOTS * EL * n_band, 2 * LANES), BF16),
+            jax.ShapeDtypeStruct((EL * n_band * n_blk, 2 * LANES), BF16),
+        ],
         in_specs=[hbm] * 2,
-        out_specs=vmem,
+        out_specs=[vmem] * 2,
         scratch_shapes=[
-            pltpu.SMEM((BANDS, SLOTS), jnp.int32),
+            pltpu.SMEM((BANDS + 1, SLOTS), jnp.int32),
             pltpu.VMEM((TAPS, C), F32),
             dma((1,)),
             pltpu.VMEM((GROUPS, FRAMES, 2, EL, GROUP_W), BF16),
@@ -330,6 +372,7 @@
             dma((GROUPS,)),
             pltpu.VMEM((BANDS, EL, 2 * LANES), BF16),
             pltpu.VMEM((EL * n_band, 2 * LANES), BF16),
+            pltpu.VMEM((n_blk * PACKED, LANES), BF16),
             dma((n_band,)),
             dma((n_band,)),
             dma((n_copies,)),
@@ -348,93 +391,44 @@
 COLUMNS = 512
 
 
-def correlate_kernel(n_blk, x, count, out, lhs, right):
-    j = pl.program_id(0)
+def correlate_kernel(left, right, out):
+    j, part = pl.program_id(0), pl.program_id(1)
     block = out.shape[3]
-    half = block // 2
-    b = lax.axis_index("blk")
-    near, along = b // 2 % 2, b // 4
-
-    def rows_of(owner):
-        d_near = (owner // 2 + near) % 2
-        d_along = (owner // 4 - along + n_blk // 4) % (n_blk // 4)
-        slot = jnp.where(d_along == 3, 4, jnp.where(d_along == 2, 6, 2 * d_along)) + d_near
-        return pl.multiple_of((owner % 2 * (n_blk // 2) + slot) * PACKED, PACKED)
-
-    def late_tile(at):
-        packed = x[pl.ds(at + block, half), :].astype(F32)
-        return packed, pltpu.roll(packed, LANES // 2, 1)
-
-    @pl.when(j == 0)
-    def _():
-        live = count[lax.axis_index("band")]
-
-        def fill(own, at, cols, used):
-            lane = lax.broadcasted_iota(jnp.int32, own.shape, 1)
-            slot = lane & 7
-            turned = jnp.where(
-                (lane & 8) == 0, pltpu.roll(own, LANES - 8, 1), -pltpu.roll(own, 8, 1)
-            )
-            keep = (slot < live) & (lane < used)
-            own, turned = jnp.where(keep, own, 0.0), jnp.where(keep, turned, 0.0)
-            for s in range(SLOTS):
-                for part, value in ((0, own), (1, turned)):
-                    to = (part * SLOTS + s) * block + at
-                    lhs[to : to + own.shape[0], cols] = jnp.where(slot == s, value, 0.0).astype(BF16)
-
-        mine = rows_of(b)
-        fill(x[pl.ds(mine, block), :].astype(F32), 0, slice(0, LANES), LANES)
-        for n, part in enumerate(late_tile(mine)):
-            fill(part, n * half, slice(LANES, 2 * LANES), (NSPEC - 8) * 16)
-
-    low = lax.broadcasted_iota(jnp.int32, (half, LANES), 1) < LANES // 2
-    for n in range(COLUMNS // block):
-        at = rows_of(j * (COLUMNS // block) + n)
-        right[n * block : (n + 1) * block, :LANES] = x[pl.ds(at, block), :]
-        for m, part in enumerate(late_tile(at)):
-            to = n * block + m * half
-            right[to : to + half, LANES:] = jnp.where(low, part, 0.0).astype(BF16)
+    rows = SLOTS * block
     y = lax.dot_general(
-        lhs[...], right[...], (((1,), (1,)), ((), ())), preferred_element_type=F32
+        left[pl.ds(pl.multiple_of(part * rows, rows), rows), :],
+        right[pl.ds(pl.multiple_of(j * COLUMNS, COLUMNS), COLUMNS), :],
+        (((1,), (1,)), ((), ())),
+        preferred_element_type=F32,
     )
     y = (y * (1.0 / NSPEC)).astype(BF16)
-    for part in range(2):
-        for s in range(SLOTS):
-            at = (part * SLOTS + s) * block
-            out[part, 0, s] = y[at : at + block]
-
-
-def correlate(x, count, n_band, n_blk):
-    block = EL * n_band
-    everyone = block * n_blk
-
-    def body(*refs):
-        correlate_kernel(n_blk, *refs)
-
+    for s in range(SLOTS):
+        out[0, 0, s] = y[s * block : (s + 1) * block]
+
+
+def correlate(left, right):
+    block, everyone = left.shape[0] // (2 * SLOTS), right.shape[0]
+    vmem = pl.BlockSpec(memory_space=pltpu.VMEM)
     return pl.pallas_call(
-        body,
-        grid=(everyone // COLUMNS,),
+        correlate_kernel,
+        grid=(everyone // COLUMNS, 2),
         out_shape=jax.ShapeDtypeStruct((2, 1, SLOTS, block, everyone), BF16),
-        in_specs=[
-            pl.BlockSpec(memory_space=pltpu.VMEM),
-            pl.BlockSpec(memory_space=pltpu.SMEM),
-        ],
-        out_specs=pl.BlockSpec((2, 1, SLOTS, block, COLUMNS), lambda j: (0, 0, 0, 0, j)),
-        scratch_shapes=[
-            pltpu.VMEM((2 * SLOTS * block, 2 * LANES), BF16),
-            pltpu.VMEM((COLUMNS, 2 * LANES), BF16),
-        ],
+        in_specs=[vmem, vmem],
+        out_specs=pl.BlockSpec(
+            (1, 1, SLOTS, block, COLUMNS), lambda j, part: (part, 0, 0, 0, j)
+        ),
         compiler_params=pltpu.CompilerParams(vmem_limit_bytes=32 * 2**20),
         name="correlate",
-    )(x, count)
+    )(left, right)
 
 
 def solution(mesh):
     n_band, n_blk = mesh.shape["band"], mesh.shape["blk"]
 
     def local(volt, band_chans, band_count):
-        x = front(volt, band_chans, n_band, n_blk)
-        return correlate(x, band_count, n_band, n_blk)
+        small = jnp.concatenate([band_chans, band_count[None]])
+        left, right = front(volt, small, n_band, n_blk)
+        return correlate(left, right)
 
     return jax.shard_map(
         local,

time: 36.4 us -> 36.1 us (level)
  local copies, waits for them, and re-layouts: 1.34 us -> 0 us
  other arithmetic: 0 us -> 0.71 us
    unnamed x4 -> x0, local copies, waits for them, and re-layouts: 1.34 us -> none
    concatenate x0 -> x1, other arithmetic: none -> 0.71 us  [local(): small = jnp.concatenate([band_chans, band_count[None]])]
where the time goes in v4:
time: 36.1 us; the launch traced here: 35.9 us
  Pallas kernels  35.2 us (98%)
  other arithmetic  0.71 us (2%)
    pallas_call x1, Pallas kernels, front(): pl.pallas_call(body, out_shape=[jax.ShapeDtypeStruct((2 * SLOTS * EL * n_...  28.9 us
    pallas_call x1, Pallas kernels, correlate(): pl.pallas_call(correlate_kernel, grid=(everyone // COLUMNS, 2), out_shape...  6.27 us

profile of v4, /device:TPU:1, one launch (start us, length us, event | category | flops | bytes accessed | tf_op | source)
XLA Modules:
  0.0 35.9 jit_solution(2524263097529225023)
XLA Ops:
  0.0 0.7 %pad_add_fusion.refs_1_ = s32[9,8]{1,0:T(8,128)S(1)} fusion(s32[1,8]{1,0:T(1,128)} %bitcast.1, s32[8,8]{1,0:T(8,128)} %param.4), kind=kLoop, calls=%fused_computation | loop fusion | flops 72 | bytes 576 | tf_op jit(solution)/shard_map/concatenate | solution.py:429
  0.7 28.9 %spectra.1 = (bf16[2048,256]{1,0:T(8,128)(2,1)S(1)}, bf16[2048,256]{1,0:T(8,128)(2,1)S(1)}) custom-call(bf16[2,16,110592]{2,1,0:T(8,128)(2,1)} %refs_0_.1, s32[9,8]{1,0:T(8,128)S(1)} %pad_add_fusion.refs_1_), custom_call_target="tpu_custom_call" | custom-call | tf_op jit(solution)/shard_map/spectra/pallas_call | solution.py:351
  29.6 6.3 %correlate.1 = bf16[2,1,8,128,2048]{4,3,2,1,0:T(8,128)(2,1)} custom-call(bf16[2048,256]{1,0:T(8,128)(2,1)S(1)} %get-tuple-element.7.left, bf16[2048,256]{1,0:T(8,128)(2,1)S(1)} %get-tuple-element.8.right), custom_call_target="tpu_custom_call" | custom-call | tf_op jit(solution)/shard_map/correlate/pallas_call | solution.py:412

commit v5 on v4

--- a/solution.py
+++ b/solution.py
@@ -19,7 +19,7 @@
 GROUPS = 4
 GROUP_W = C // GROUPS
 CHUNK = 512
-N_CENTRE = 4
+N_CENTRE = 2
 N_CHUNK = C // CHUNK
 MESH = pl.DeviceIdType.MESH
 F32, BF16 = jnp.float32, jnp.bfloat16
@@ -133,7 +133,7 @@
 
     lax.fori_loop(0, N_CHUNK, build, 0)
 
-    def weigh(chunk, lhs):
+    def weigh(chunk, lhs, before=None):
         group = chunk // (GROUP_W // CHUNK)
         for part in range(CHUNK // LANES):
             k = pl.multiple_of(chunk * CHUNK + part * LANES, LANES)
@@ -144,6 +144,8 @@
             ]
             taps = [taps[p] if p in CENTRE else taps[p].astype(BF16) for p in range(TAPS)]
             column = slice(part * LANES, (part + 1) * LANES)
+            if before is not None:
+                piece(before[0], before[1], part)
             for comp in range(2):
                 side, mid = [None] * NSPEC, [None] * NSPEC
                 for f in range(FRAMES):
@@ -164,9 +166,15 @@
                         lhs[at : at + EL, column] = hi
                         lhs[ROWS + at : ROWS + at + EL, column] = lo
 
-    def transform(chunk, lhs):
-        r = jnp.dot(lhs[...], table[chunk], preferred_element_type=F32)
-        total[...] += (r[:ROWS, LANES:] + r[ROWS:, :LANES]) + r[:ROWS, :LANES]
+    def piece(chunk, lhs, n):
+        count = ROWS // 2
+        at = n * count
+        if n < 2:
+            r = jnp.dot(lhs[at : at + count, :], table[chunk], preferred_element_type=F32)
+            total[at : at + count, :] += r[:, :LANES] + r[:, LANES:]
+        else:
+            r = jnp.dot(lhs[at : at + count, :], table[chunk, :, :LANES], preferred_element_type=F32)
+            total[at - ROWS : at - ROWS + count, :] += r
 
     def wait_group(group):
         pltpu.make_async_copy(samples.at[group], samples.at[group], sems.at[group]).wait()
@@ -178,10 +186,8 @@
 
     def two_chunks(i, carry):
         first = i * 2
-        weigh(first, lhs_a)
-        transform(lax.max(first - 1, 0), lhs_b)
-        weigh(first + 1, lhs_b)
-        transform(first, lhs_a)
+        weigh(first, lhs_a, (lax.max(first - 1, 0), lhs_b))
+        weigh(first + 1, lhs_b, (first, lhs_a))
         return carry
 
     for group in range(GROUPS):
@@ -189,7 +195,8 @@
             fetch_group(group + 2)
         wait_group(group)
         lax.fori_loop(group * per_group // 2, (group + 1) * per_group // 2, two_chunks, 0)
-    transform(N_CHUNK - 1, lhs_b)
+    for n in range(4):
+        piece(N_CHUNK - 1, lhs_b, n)
 
     is_real = (lax.broadcasted_iota(jnp.int32, (EL, LANES), 1) & 8) == 0
     y = []
@@ -391,19 +398,35 @@
 COLUMNS = 512
 
 
-def correlate_kernel(left, right, out):
-    j, part = pl.program_id(0), pl.program_id(1)
+def correlate_kernel(left, right, out, done, sems):
     block = out.shape[3]
-    rows = SLOTS * block
-    y = lax.dot_general(
-        left[pl.ds(pl.multiple_of(part * rows, rows), rows), :],
-        right[pl.ds(pl.multiple_of(j * COLUMNS, COLUMNS), COLUMNS), :],
-        (((1,), (1,)), ((), ())),
-        preferred_element_type=F32,
-    )
-    y = (y * (1.0 / NSPEC)).astype(BF16)
-    for s in range(SLOTS):
-        out[0, 0, s] = y[s * block : (s + 1) * block]
+    everyone = right.shape[0]
+    copies = []
+    for at in range(0, everyone, COLUMNS):
+        cols = slice(at, at + COLUMNS)
+        for first, last in ((0, 4), (4, 8), (8, 16)) if at == 0 else ((0, 8), (8, 16)):
+            y = lax.dot_general(
+                left[first * block : last * block, :],
+                right[cols, :],
+                (((1,), (1,)), ((), ())),
+                preferred_element_type=F32,
+            )
+            y = (y * (1.0 / NSPEC)).astype(BF16)
+            for n in range(first, last):
+                part, s = n // SLOTS, n % SLOTS
+                done[part, s, :, cols] = y[(n - first) * block : (n - first + 1) * block]
+                if n % 2:
+                    pair = pl.ds(s - 1, 2)
+                    copies.append(
+                        pltpu.make_async_copy(
+                            done.at[part, pair, :, pl.ds(at, COLUMNS)],
+                            out.at[part, 0, pair, :, pl.ds(at, COLUMNS)],
+                            sems.at[len(copies)],
+                        )
+                    )
+                    copies[-1].start()
+    for copy in copies:
+        copy.wait()
 
 
 def correlate(left, right):
@@ -411,13 +434,14 @@
     vmem = pl.BlockSpec(memory_space=pltpu.VMEM)
     return pl.pallas_call(
         correlate_kernel,
-        grid=(everyone // COLUMNS, 2),
         out_shape=jax.ShapeDtypeStruct((2, 1, SLOTS, block, everyone), BF16),
         in_specs=[vmem, vmem],
-        out_specs=pl.BlockSpec(
-            (1, 1, SLOTS, block, COLUMNS), lambda j, part: (part, 0, 0, 0, j)
-        ),
-        compiler_params=pltpu.CompilerParams(vmem_limit_bytes=32 * 2**20),
+        out_specs=pl.BlockSpec(memory_space=pltpu.HBM),
+        scratch_shapes=[
+            pltpu.VMEM((2, SLOTS, block, everyone), BF16),
+            pltpu.SemaphoreType.DMA((SLOTS * everyone // COLUMNS,)),
+        ],
+        compiler_params=pltpu.CompilerParams(vmem_limit_bytes=48 * 2**20),
         name="correlate",
     )(left, right)
 

time: 36.1 us -> 33.2 us (0.920)
  Pallas kernels: 35.2 us -> 32.3 us
    pallas_call x1, Pallas kernels: 6.27 us -> 3.81 us  [correlate(): pl.pallas_call(correlate_kernel, out_shape=jax.ShapeDtypeStruct((2, 1, SL...]
    pallas_call x1, Pallas kernels: 28.9 us -> 28.5 us  [front(): pl.pallas_call(body, out_shape=[jax.ShapeDtypeStruct((2 * SLOTS * EL * n_...]
where the time goes in v5:
time: 33.2 us; the launch traced here: 33 us
  Pallas kernels  32.3 us (97%)
  other arithmetic  0.71 us (2%)
    pallas_call x1, Pallas kernels, front(): pl.pallas_call(body, out_shape=[jax.ShapeDtypeStruct((2 * SLOTS * EL * n_...  28.5 us
    pallas_call x1, Pallas kernels, correlate(): pl.pallas_call(correlate_kernel, out_shape=jax.ShapeDtypeStruct((2, 1, SL...  3.81 us
    concatenate x1, other arithmetic, local(): small = jnp.concatenate([band_chans, band_count[None]])  0.71 us

profile of v5, /device:TPU:1, one launch (start us, length us, event | category | flops | bytes accessed | tf_op | source)
XLA Modules:
  0.0 33.0 jit_solution(3600833258945765627)
XLA Ops:
  0.0 0.7 %pad_add_fusion.refs_1_ = s32[9,8]{1,0:T(8,128)S(1)} fusion(s32[1,8]{1,0:T(1,128)} %bitcast.1, s32[8,8]{1,0:T(8,128)} %param.4), kind=kLoop, calls=%fused_computation | loop fusion | flops 72 | bytes 576 | tf_op jit(solution)/shard_map/concatenate | solution.py:453
  0.7 28.5 %spectra.1 = (bf16[2048,256]{1,0:T(8,128)(2,1)S(1)}, bf16[2048,256]{1,0:T(8,128)(2,1)S(1)}) custom-call(bf16[2,16,110592]{2,1,0:T(8,128)(2,1)} %refs_0_.1, s32[9,8]{1,0:T(8,128)S(1)} %pad_add_fusion.refs_1_), custom_call_target="tpu_custom_call" | custom-call | tf_op jit(solution)/shard_map/spectra/pallas_call | solution.py:358
  29.2 3.8 %correlate.1 = bf16[2,1,8,128,2048]{4,3,2,1,0:T(8,128)(2,1)} custom-call(bf16[2048,256]{1,0:T(8,128)(2,1)S(1)} %get-tuple-element.7.left, bf16[2048,256]{1,0:T(8,128)(2,1)S(1)} %get-tuple-element.8.right), custom_call_target="tpu_custom_call" | custom-call | tf_op jit(solution)/shard_map/correlate/pallas_call | solution.py:435

commit v6 on v5

--- a/solution.py
+++ b/solution.py
@@ -82,7 +82,7 @@
 
 
 def front_kernel(
-    n_band, n_blk, volt, chans_hbm, left, right, chans, taper, small_sem, samples, base_c, base_s,
+    n_band, n_blk, volt, chans_hbm, count_hbm, left, right, chans, count, taper, small_sem, samples, base_c, base_s,
     step_c, step_s, table, lhs_a, lhs_b, total, sems, z, turned, x, *comm_sems
 ):
     def fetch(group, frame):
@@ -96,13 +96,18 @@
         for frame in range(FRAMES):
             fetch(group, frame).start()
 
-    small = pltpu.make_async_copy(chans_hbm, chans, small_sem.at[0])
-    small.start()
+    small = [
+        pltpu.make_async_copy(chans_hbm, chans, small_sem.at[0]),
+        pltpu.make_async_copy(count_hbm, count, small_sem.at[1]),
+    ]
+    for copy in small:
+        copy.start()
     fetch_group(0)
     greet(n_band, n_blk)
     fetch_group(1)
     fill_taper(taper)
-    small.wait()
+    for copy in small:
+        copy.wait()
 
     lane = lax.broadcasted_iota(jnp.int32, (8, LANES), 1)
     key = ((lane >> 4) << 3) + (lane & 7)
@@ -147,24 +152,21 @@
             if before is not None:
                 piece(before[0], before[1], part)
             for comp in range(2):
-                side, mid = [None] * NSPEC, [None] * NSPEC
-                for f in range(FRAMES):
-                    x = samples[group, f, comp, :, pl.ds(in_group, LANES)]
-                    wide = x.astype(F32)
-                    for t in range(max(0, f - TAPS + 1), min(NSPEC - 1, f) + 1):
-                        p = f - t
-                        if p in CENTRE:
-                            term = taps[p] * wide
-                            mid[t] = term if mid[t] is None else mid[t] + term
-                        else:
-                            term = taps[p] * x
-                            side[t] = term if side[t] is None else side[t] + term
-                    if f >= TAPS - 1:
-                        t = f - TAPS + 1
-                        hi, lo = split(mid[t] + side[t].astype(F32))
-                        at = (comp * NSPEC + t) * EL
-                        lhs[at : at + EL, column] = hi
-                        lhs[ROWS + at : ROWS + at + EL, column] = lo
+                x = [samples[group, f, comp, :, pl.ds(in_group, LANES)] for f in range(FRAMES)]
+                for t in range(NSPEC):
+                    sides = []
+                    for order in (OUTER[: len(OUTER) // 2], OUTER[: len(OUTER) // 2 - 1 : -1]):
+                        side = taps[order[0]] * x[t + order[0]]
+                        for p in order[1:]:
+                            side = side + taps[p] * x[t + p]
+                        sides.append(side)
+                    y = sides[0].astype(F32) + sides[1].astype(F32)
+                    for p in CENTRE:
+                        y = y + taps[p] * x[t + p].astype(F32)
+                    hi, lo = split(y)
+                    at = (comp * NSPEC + t) * EL
+                    lhs[at : at + EL, column] = hi
+                    lhs[ROWS + at : ROWS + at + EL, column] = lo
 
     def piece(chunk, lhs, n):
         count = ROWS // 2
@@ -216,7 +218,7 @@
                     moved = pltpu.roll(moved, shift, 1)
                 out = jnp.where(place == t - tile * 8, moved, out)
             z[g, :, tile * LANES : (tile + 1) * LANES] = out.astype(BF16)
-    share(n_band, n_blk, z, turned, x, chans, left, right, *comm_sems)
+    share(n_band, n_blk, z, turned, x, count, left, right, *comm_sems)
 
 
 def places(n_band, n_blk):
@@ -271,7 +273,7 @@
 
 
 def share(
-    n_band, n_blk, z, turned, x, chans, left, right, ct_send, ct_recv, ag_send, ag_recv, fw_send,
+    n_band, n_blk, z, turned, x, count, left, right, ct_send, ct_recv, ag_send, ag_recv, fw_send,
     fw_recv, here,
 ):
     g, b, sibling, chip = places(n_band, n_blk)
@@ -321,7 +323,7 @@
         remote(own, slots(core, slot_of(-da, dn)), ag_send.at[n], ag_recv.at[n], (g, chip(da, dn)))
         for n, (da, dn) in enumerate(STEPS)
     ]
-    fill_left(left, turned, chans[BANDS, g])
+    fill_left(left, turned, count[g])
     unpack(core, 0, 1)
     onward = []
     for n, (da, dn) in enumerate(STEPS):
@@ -346,7 +348,7 @@
         copy.wait_send()
 
 
-def front(volt, chans, n_band, n_blk):
+def front(volt, chans, count, n_band, n_blk):
     hbm = pl.BlockSpec(memory_space=pltpu.HBM)
     dma = pltpu.SemaphoreType.DMA
     n_copies = len(STEPS) + len(PASSED)
@@ -361,12 +363,13 @@
             jax.ShapeDtypeStruct((2 * SLOTS * EL * n_band, 2 * LANES), BF16),
             jax.ShapeDtypeStruct((EL * n_band * n_blk, 2 * LANES), BF16),
         ],
-        in_specs=[hbm] * 2,
+        in_specs=[hbm] * 3,
         out_specs=[vmem] * 2,
         scratch_shapes=[
-            pltpu.SMEM((BANDS + 1, SLOTS), jnp.int32),
+            pltpu.SMEM((BANDS, SLOTS), jnp.int32),
+            pltpu.SMEM((BANDS,), jnp.int32),
             pltpu.VMEM((TAPS, C), F32),
-            dma((1,)),
+            dma((2,)),
             pltpu.VMEM((GROUPS, FRAMES, 2, EL, GROUP_W), BF16),
             pltpu.VMEM((LANES, LANES), F32),
             pltpu.VMEM((LANES, LANES), F32),
@@ -392,7 +395,7 @@
             vmem_limit_bytes=48 * 2**20, collective_id=0, has_side_effects=True
         ),
         name="spectra",
-    )(volt, chans)
+    )(volt, chans, count)
 
 
 COLUMNS = 512
@@ -450,8 +453,10 @@
     n_band, n_blk = mesh.shape["band"], mesh.shape["blk"]
 
     def local(volt, band_chans, band_count):
-        small = jnp.concatenate([band_chans, band_count[None]])
-        left, right = front(volt, small, n_band, n_blk)
+        chans, count = (
+            pltpu.with_memory_space_constraint(a, pltpu.HBM) for a in (band_chans, band_count)
+        )
+        left, right = front(volt, chans, count, n_band, n_blk)
         return correlate(left, right)
 
     return jax.shard_map(

time: 33.2 us -> 32.9 us (level)
  other arithmetic: 0.71 us -> 0 us
  Pallas kernels: 32.3 us -> 32.7 us
    concatenate x1 -> x0, other arithmetic: 0.71 us -> none  [local(): small = jnp.concatenate([band_chans, band_count[None]])]
    pallas_call x1, Pallas kernels: 28.5 us -> 28.9 us  [front(): pl.pallas_call(body, out_shape=[jax.ShapeDtypeStruct((2 * SLOTS * EL * n_...]
where the time goes in v6:
time: 32.9 us; the launch traced here: 32.7 us
  Pallas kernels  32.7 us (99%)
    pallas_call x1, Pallas kernels, front(): pl.pallas_call(body, out_shape=[jax.ShapeDtypeStruct((2 * SLOTS * EL * n_...  28.9 us
    pallas_call x1, Pallas kernels, correlate(): pl.pallas_call(correlate_kernel, out_shape=jax.ShapeDtypeStruct((2, 1, SL...  3.8 us

profile of v6, /device:TPU:1, one launch (start us, length us, event | category | flops | bytes accessed | tf_op | source)
XLA Modules:
  0.0 32.7 jit_solution(6434686324062760433)
XLA Ops:
  0.0 28.9 %spectra.1 = (bf16[2048,256]{1,0:T(8,128)(2,1)S(1)}, bf16[2048,256]{1,0:T(8,128)(2,1)S(1)}) custom-call(bf16[2,16,110592]{2,1,0:T(8,128)(2,1)} %refs_0_.1, s32[8,8]{1,0:T(8,128)} %refs_1_.1, s32[8]{0:T(128)} %refs_2_.1), custom_call_target="tpu_custom_call" | custom-call | tf_op jit(solution)/shard_map/spectra/pallas_call | solution.py:360
  28.9 3.8 %correlate.1 = bf16[2,1,8,128,2048]{4,3,2,1,0:T(8,128)(2,1)} custom-call(bf16[2048,256]{1,0:T(8,128)(2,1)S(1)} %get-tuple-element.7.left, bf16[2048,256]{1,0:T(8,128)(2,1)S(1)} %get-tuple-element.8.right), custom_call_target="tpu_custom_call" | custom-call | tf_op jit(solution)/shard_map/correlate/pallas_call | solution.py:438

commit v7 on v6

--- a/solution.py
+++ b/solution.py
@@ -141,8 +141,8 @@
     def weigh(chunk, lhs, before=None):
         group = chunk // (GROUP_W // CHUNK)
         for part in range(CHUNK // LANES):
-            k = pl.multiple_of(chunk * CHUNK + part * LANES, LANES)
-            in_group = pl.multiple_of(k - group * GROUP_W, LANES)
+            k = chunk * CHUNK + part * LANES
+            in_group = k - group * GROUP_W
             taps = [
                 jnp.broadcast_to(taper[p : p + 1, pl.ds(k, LANES)], (EL, LANES))
                 for p in range(TAPS)
@@ -182,23 +182,19 @@
         pltpu.make_async_copy(samples.at[group], samples.at[group], sems.at[group]).wait()
 
     total[...] = jnp.zeros_like(total)
-    lhs_b[...] = jnp.zeros_like(lhs_b)
-
     per_group = GROUP_W // CHUNK
-
-    def two_chunks(i, carry):
-        first = i * 2
-        weigh(first, lhs_a, (lax.max(first - 1, 0), lhs_b))
-        weigh(first + 1, lhs_b, (first, lhs_a))
-        return carry
-
-    for group in range(GROUPS):
-        if group + 2 < GROUPS:
-            fetch_group(group + 2)
-        wait_group(group)
-        lax.fori_loop(group * per_group // 2, (group + 1) * per_group // 2, two_chunks, 0)
+    held, other, before = lhs_a, lhs_b, None
+    for chunk in range(N_CHUNK):
+        if chunk % per_group == 0:
+            group = chunk // per_group
+            if group + 2 < GROUPS:
+                fetch_group(group + 2)
+            wait_group(group)
+        weigh(chunk, held, before)
+        before = (chunk, held)
+        held, other = other, held
     for n in range(4):
-        piece(N_CHUNK - 1, lhs_b, n)
+        piece(*before, n)
 
     is_real = (lax.broadcasted_iota(jnp.int32, (EL, LANES), 1) & 8) == 0
     y = []

time: 32.9 us -> 32.6 us (level)
  no operation moved by 1% of the time
where the time goes in v7:
time: 32.6 us; the launch traced here: 32.5 us
  Pallas kernels  32.5 us (100%)
    pallas_call x1, Pallas kernels, front(): pl.pallas_call(body, out_shape=[jax.ShapeDtypeStruct((2 * SLOTS * EL * n_...  28.7 us
    pallas_call x1, Pallas kernels, correlate(): pl.pallas_call(correlate_kernel, out_shape=jax.ShapeDtypeStruct((2, 1, SL...  3.81 us

profile of v7, /device:TPU:1, one launch (start us, length us, event | category | flops | bytes accessed | tf_op | source)
XLA Modules:
  0.0 32.5 jit_solution(13142159085411459503)
XLA Ops:
  0.0 28.7 %spectra.1 = (bf16[2048,256]{1,0:T(8,128)(2,1)S(1)}, bf16[2048,256]{1,0:T(8,128)(2,1)S(1)}) custom-call(bf16[2,16,110592]{2,1,0:T(8,128)(2,1)} %refs_0_.1, s32[8,8]{1,0:T(8,128)} %refs_1_.1, s32[8]{0:T(128)} %refs_2_.1), custom_call_target="tpu_custom_call" | custom-call | tf_op jit(solution)/shard_map/spectra/pallas_call | solution.py:356
  28.7 3.8 %correlate.1 = bf16[2,1,8,128,2048]{4,3,2,1,0:T(8,128)(2,1)} custom-call(bf16[2048,256]{1,0:T(8,128)(2,1)S(1)} %get-tuple-element.7.left, bf16[2048,256]{1,0:T(8,128)(2,1)S(1)} %get-tuple-element.8.right), custom_call_target="tpu_custom_call" | custom-call | tf_op jit(solution)/shard_map/correlate/pallas_call | solution.py:434

commit v8 on v7

--- a/solution.py
+++ b/solution.py
@@ -246,6 +246,7 @@
     g, b, sibling, chip = places(n_band, n_blk)
     peers = [((g + d) % n_band, b) for d in range(1, n_band)]
     peers += [(g, chip(*step)) for step in STEPS] + [(g, sibling)]
+    peers += [(g, chip(da, 0) + sibling - b) for da in (1, -1)]
     barrier = pltpu.get_barrier_semaphore()
     for peer in peers:
         pl.semaphore_signal(barrier, inc=1, device_id=peer, device_id_type=MESH)
@@ -273,7 +274,7 @@
     fw_recv, here,
 ):
     g, b, sibling, chip = places(n_band, n_blk)
-    pl.semaphore_wait(pltpu.get_barrier_semaphore(), n_band - 1 + len(STEPS) + 1)
+    pl.semaphore_wait(pltpu.get_barrier_semaphore(), n_band - 1 + len(STEPS) + 3)
     block = EL * n_band
     half = block // 2
     core = b % 2
@@ -327,27 +328,28 @@
         if n in PASSED:
             m = len(STEPS) + len(onward)
             came, goes = slots(core, slot_of(-da, dn)), slots(core, slot_of(-2 * da, dn))
-            onward.append(remote(came, goes, ag_send.at[m], ag_recv.at[m], (g, chip(da, 0))))
+            for n_core, to in enumerate((chip(da, 0), chip(da, 0) + 1 - 2 * core)):
+                onward.append(
+                    remote(came, goes, ag_send.at[m + n_core], ag_recv.at[m + n_core], (g, to))
+                )
     n_near = len(STEPS) + 1
-    near, far = slots(core, 0, n_near), slots(core, n_near, 2)
+    near = slots(core, 0, n_near)
     near_copy = remote(near, near, fw_send.at[0], fw_recv.at[0], (g, sibling))
     unpack(core, 1, n_near - 1)
     near_copy.wait_recv()
     unpack(1 - core, 0, n_near)
     for copy in onward:
         copy.wait_recv()
-    far_copy = remote(far, far, fw_send.at[1], fw_recv.at[1], (g, sibling))
     unpack(core, n_near, 2)
-    far_copy.wait_recv()
     unpack(1 - core, n_near, 2)
-    for copy in turns + sends + onward + [near_copy, far_copy]:
+    for copy in turns + sends + onward + [near_copy]:
         copy.wait_send()
 
 
 def front(volt, chans, count, n_band, n_blk):
     hbm = pl.BlockSpec(memory_space=pltpu.HBM)
     dma = pltpu.SemaphoreType.DMA
-    n_copies = len(STEPS) + len(PASSED)
+    n_copies = len(STEPS) + 2 * len(PASSED)
     vmem = pl.BlockSpec(memory_space=pltpu.VMEM)
 
     def body(*refs):

time: 32.6 us -> 31.7 us (0.972)
  Pallas kernels: 32.5 us -> 31.6 us
    pallas_call x1, Pallas kernels: 28.7 us -> 27.8 us  [front(): pl.pallas_call(body, out_shape=[jax.ShapeDtypeStruct((2 * SLOTS * EL * n_...]
where the time goes in v8:
time: 31.7 us; the launch traced here: 31.6 us
  Pallas kernels  31.6 us (100%)
    pallas_call x1, Pallas kernels, front(): pl.pallas_call(body, out_shape=[jax.ShapeDtypeStruct((2 * SLOTS * EL * n_...  27.8 us
    pallas_call x1, Pallas kernels, correlate(): pl.pallas_call(correlate_kernel, out_shape=jax.ShapeDtypeStruct((2, 1, SL...  3.81 us

profile of v8, /device:TPU:1, one launch (start us, length us, event | category | flops | bytes accessed | tf_op | source)
XLA Modules:
  0.0 31.6 jit_solution(9594516230738143457)
XLA Ops:
  0.0 27.8 %spectra.1 = (bf16[2048,256]{1,0:T(8,128)(2,1)S(1)}, bf16[2048,256]{1,0:T(8,128)(2,1)S(1)}) custom-call(bf16[2,16,110592]{2,1,0:T(8,128)(2,1)} %refs_0_.1, s32[8,8]{1,0:T(8,128)} %refs_1_.1, s32[8]{0:T(128)} %refs_2_.1), custom_call_target="tpu_custom_call" | custom-call | tf_op jit(solution)/shard_map/spectra/pallas_call | solution.py:358
  27.8 3.8 %correlate.1 = bf16[2,1,8,128,2048]{4,3,2,1,0:T(8,128)(2,1)} custom-call(bf16[2048,256]{1,0:T(8,128)(2,1)S(1)} %get-tuple-element.7.left, bf16[2048,256]{1,0:T(8,128)(2,1)S(1)} %get-tuple-element.8.right), custom_call_target="tpu_custom_call" | custom-call | tf_op jit(solution)/shard_map/correlate/pallas_call | solution.py:436
